TPU v7x, 256 devices: a whole 4x4x8 slice. The times are simulated.
256 devices in a mesh: pb: 16 (over x_lo, z), ka: 16 (over x_hi, y, core).
Axes of the slice: x: 4 (x_hi: 2, x_lo: 2; x = x_hi * 2 + x_lo), y: 4, z: 8, core: 2. Of those that a mesh axis runs over, the one named last changes fastest.
Arguments:
- query_saved: bfloat16 [8192, 1024], P(('pb', 'ka')), may hold values from -6 to 6
- key_saved: bfloat16 [16384, 1024], P(('ka', 'pb')), may hold values from -6 to 6
- value_saved: bfloat16 [16384, 1024], P(('ka', 'pb')), may hold values from -6 to 6
- out_grad: bfloat16 [8192, 1024], P(('pb', 'ka')), may hold values from -768 to 768
- log_norm: bfloat16 [16, 8192], P(None, ('pb', 'ka')), as said below
- row_delta: bfloat16 [16, 8192], P(None, ('pb', 'ka')), may hold values from -1536 to 1536
- weight_query: bfloat16 [1024, 1024], replicated, may hold values from -0.1875 to 0.1875
- weight_key: bfloat16 [1024, 1024], replicated, may hold values from -0.1875 to 0.1875
- weight_value: bfloat16 [1024, 1024], replicated, may hold values from -0.1875 to 0.1875
Outputs:
- dx_query: bfloat16 [8192, 1024], P(('pb', 'ka'))
- dx_keyvalue: bfloat16 [16384, 1024], P(('ka', 'pb'))
Inputs may be any that keep to these rules, and one draw needn't show every extreme that they name: `log_norm`: each entry lies within 2 of 0.5 plus the natural logarithm of 16384.
All inputs are finite; a program needn't handle non-finite values.
Results may differ from a plain program's by a relative error of at most 0.008.
Values may be sent and summed in bfloat16 or wider, within the bound.
A program may use at most 128 MiB of HBM per device.

v0:
```python
import jax
import jax.numpy as jnp
from jax import lax
from jax.sharding import PartitionSpec as P

HEAD_DIM = 64


def turned_gather(arrays, axis, dims):
    turned = [jnp.moveaxis(a, dim, 0) for a, dim in zip(arrays, dims)]
    both = jnp.concatenate([t.reshape(len(t), -1) for t in turned], axis=1)
    whole, at, outs = (lax.all_gather(both, axis, axis=0, tiled=True), 0, [])
    for t, dim in zip(turned, dims):
        share = whole[:, at : at + t[0].size].reshape(-1, *t.shape[1:])
        outs.append(jnp.moveaxis(share, 0, dim))
        at += t[0].size
    return tuple(outs)


def in_one_piece(arrays, axis, dim, along):
    both = jnp.concatenate(arrays, axis=along)
    whole, at, outs = (lax.all_gather(both, axis, axis=dim, tiled=True), 0, [])
    for a in arrays:
        outs.append(lax.slice_in_dim(whole, at, at + a.shape[along], axis=along))
        at += a.shape[along]
    return tuple(outs)


def cut_along(array, dim, size):
    before, after = (array.shape[:dim], array.shape[dim + 1 :])
    return jnp.moveaxis(array.reshape(*before, size, -1, *after), dim, 0)


def summed_on_arrival(array, axis, dim):
    pieces = cut_along(array, dim, lax.axis_size(axis))
    arrived = lax.all_to_all(pieces, axis, split_axis=0, concat_axis=0, tiled=True)
    return arrived.sum(axis=0)


def project(grads, weights):
    contract = (((1,), (1,)), ((), ()))
    upper = grads.astype(jnp.bfloat16)
    lower = (grads - upper.astype(jnp.float32)).astype(jnp.bfloat16)
    first = lax.dot_general(upper, weights, contract, preferred_element_type=jnp.float32)
    return first + lax.dot_general(lower, weights, contract, preferred_element_type=jnp.float32)


def local(
    query_saved,
    key_saved,
    value_saved,
    out_grad,
    log_norm,
    row_delta,
    weight_query,
    weight_key,
    weight_value,
):
    query_block, grad_out_block, norm_block, delta_block = turned_gather(
        (query_saved, out_grad, log_norm, row_delta), "ka", (0, 0, 1, 1)
    )
    key_block, value_block = in_one_piece((key_saved, value_saved), "pb", 0, 1)
    query_rows = query_block.shape[0]
    key_rows = key_block.shape[0]
    model_width = query_block.shape[1]
    pair_width = 2 * HEAD_DIM
    pair_count = model_width // pair_width
    score_scale = 1.0 / HEAD_DIM**0.5

    def columns(source, row_count, column):
        return lax.dynamic_slice_in_dim(source, column, pair_width, 1).reshape(
            row_count, 2, HEAD_DIM
        )

    def head_pair(pair_index, totals):
        grad_query, grad_key, grad_value = totals
        column = pair_index * pair_width
        queries = columns(query_block, query_rows, column)
        grads_out = columns(grad_out_block, query_rows, column)
        keys_pair = columns(key_block, key_rows, column)
        values_pair = columns(value_block, key_rows, column)
        norm_pair = lax.dynamic_slice_in_dim(norm_block, pair_index * 2, 2, 0).astype(jnp.float32)
        delta_pair = lax.dynamic_slice_in_dim(delta_block, pair_index * 2, 2, 0).astype(jnp.float32)
        scores = (
            jnp.einsum("qhd,khd->hqk", queries, keys_pair, preferred_element_type=jnp.float32)
            * score_scale
        )
        probs = jnp.exp(scores - norm_pair[:, :, None])
        probs_b = probs.astype(jnp.bfloat16)
        grad_probs = jnp.einsum(
            "qhd,khd->hqk", grads_out, values_pair, preferred_element_type=jnp.float32
        )
        grad_scores = probs * (grad_probs - delta_pair[:, :, None])
        grad_scores_b = grad_scores.astype(jnp.bfloat16)
        value_part = jnp.einsum(
            "hqk,qhd->khd", probs_b, grads_out, preferred_element_type=jnp.float32
        )
        key_part = (
            jnp.einsum("hqk,qhd->khd", grad_scores_b, queries, preferred_element_type=jnp.float32)
            * score_scale
        )
        query_part = (
            jnp.einsum("hqk,khd->qhd", grad_scores_b, keys_pair, preferred_element_type=jnp.float32)
            * score_scale
        )
        grad_query = lax.dynamic_update_slice_in_dim(
            grad_query, query_part.reshape(query_rows, pair_width), column, 1
        )
        grad_key = lax.dynamic_update_slice_in_dim(
            grad_key, key_part.reshape(key_rows, pair_width), column, 1
        )
        grad_value = lax.dynamic_update_slice_in_dim(
            grad_value, value_part.reshape(key_rows, pair_width), column, 1
        )
        return (grad_query, grad_key, grad_value)

    start_totals = (
        jnp.zeros((query_rows, model_width), jnp.float32),
        jnp.zeros((key_rows, model_width), jnp.float32),
        jnp.zeros((key_rows, model_width), jnp.float32),
    )
    grad_query, grad_key, grad_value = lax.fori_loop(0, pair_count, head_pair, start_totals)
    query_owned = summed_on_arrival(grad_query, "ka", 0)
    dx_query = project(query_owned, weight_query).astype(jnp.bfloat16)
    combined = lax.psum_scatter(
        project(grad_key, weight_key) + project(grad_value, weight_value),
        "pb",
        scatter_dimension=0,
        tiled=True,
    )
    return (dx_query, combined.astype(jnp.bfloat16))


def solution(mesh):
    in_specs = (
        P(("pb", "ka"), None),
        P(("ka", "pb"), None),
        P(("ka", "pb"), None),
        P(("pb", "ka"), None),
        P(None, ("pb", "ka")),
        P(None, ("pb", "ka")),
        P(),
        P(),
        P(),
    )
    out_specs = (P(("pb", "ka"), None), P(("ka", "pb"), None))
    return jax.shard_map(local, mesh=mesh, in_specs=in_specs, out_specs=out_specs, check_vma=False)
```

profile of v0, /device:TPU:1, one launch (start us, length us, event | category | flops | bytes accessed | tf_op | source)
XLA Modules:
  0.0 404.5 jit_solution(9012038801444928533)
XLA Ops:
  12.4 55.4 %all-gather.5.cloned.1.call-done = bf16[512,2080]{1,0:T(8,128)(2,1)} async-done(((bf16[32,2080]{1,0:T(8,128)(2,1)}), bf16[512,2080]{1,0:T(8,128)(2,1)}) %all-gather.5.cloned.1.call-update) | async-done | bytes 2129936 | tf_op jit(solution)/shard_map/all_gather | solution.py:12
  69.0 3.1 fusion.20
  72.1 62.5 %all-gather.3.cloned.1.call-done = bf16[1024,2048]{1,0:T(8,128)(2,1)} async-done(((bf16[64,2048]{1,0:T(8,128)(2,1)}), bf16[1024,2048]{1,0:T(8,128)(2,1)}) %all-gather.3.cloned.1.call-update) | async-done | bytes 4194320 | tf_op jit(solution)/shard_map/all_gather | solution.py:22
  134.6 4.6 %fusion.19 = (bf16[1024,1024]{1,0:T(8,128)(2,1)}, bf16[1024,1024]{1,0:T(8,128)(2,1)}) fusion(bf16[1024,2048]{1,0:T(8,128)(2,1)} %all-gather.3.cloned.1.call-done), kind=kLoop, calls=%fused_computation.39 | loop fusion | bytes 8388608 | tf_op jit(solution)/shard_map/slice | solution.py:24
  145.7 145.1 %while.17 = (s32[]{:T(128)}, f32[512,1024]{1,0:T(8,128)}, f32[1024,1024]{0,1:T(8,128)}, f32[1024,1024]{0,1:T(8,128)}, bf16[1024,1024]{1,0:T(8,128)(2,1)}, /*inde...) while((s32[]{:T(128)}, f32[512,1024]{1,0:T(8,128)}, ...), condition=%wide.region_1.0_spmd, body=%wide.region_0.0_spmd.sunk | while | flops 679675904 | bytes 44589392 | solution.py:122
  152.8 3.4 multiply_convert_fusion.2
  159.2 3.1 fusion.64
  171.0 3.4 multiply_convert_fusion.2
  177.3 3.1 fusion.64
  189.1 3.4 multiply_convert_fusion.2
  195.4 3.1 fusion.64
  207.2 3.4 multiply_convert_fusion.2
  213.6 3.1 fusion.64
  225.3 3.4 multiply_convert_fusion.2
  231.7 3.1 fusion.64
  243.5 3.4 multiply_convert_fusion.2
  249.8 3.1 fusion.64
  261.6 3.4 multiply_convert_fusion.2
  267.9 3.1 fusion.64
  279.7 3.4 multiply_convert_fusion.2
  286.1 3.1 fusion.64
  290.8 4.7 %fusion.14 = f32[1024,1024]{1,0:T(8,128)S(1)} fusion(bf16[1024,1024]{1,0:T(8,128)(2,1)S(1)} %copy-done, f32[1024,1024]{0,1:T(8,128)} %get-tuple-element.174), kind=kOutput, calls=%fused_computation.30 | convolution fusion | flops 2148532224 | bytes 10485760 | tf_op jit(solution)/shard_map/dot_general | solution.py:44
  300.8 4.4 %add_add_fusion = f32[1024,1024]{1,0:T(8,128)} fusion(f32[1024,1024]{1,0:T(8,128)S(1)} %fusion.9, f32[1024,1024]{1,0:T(8,128)S(1)} %fusion.14, f32[1024,1024]{1,0:T(8,128)S(1)} %fusion.8, bf16[1024,1024]{1,0:T(8,128)(2,1)S(1)} %copy-done.5, f32[1024,1024]{0,1:T(8,128)S(1)} %copy-done.3), kind=kOutput, calls=%fused_computation.20 | convolution fusion | flops 2151677952 | bytes 23068672 | tf_op jit(solution)/shard_map/dot_general | solution.py:44
  305.2 84.1 %all_to_all.5 = f32[16,32,1024]{2,1,0:T(8,128)} all-to-all(f32[16,32,1024]{2,1,0:T(8,128)} %bitcast.77), channel_id=1, replica_groups=mesh['pb'=16,'ka'=16] {'ka'}, dimensions={0} | all-to-all | bytes 4194304 | tf_op jit(solution)/shard_map/all_to_all | solution.py:36
  (191 shorter events, 119.5 us)
Async XLA Ops:
  7.2 283.6 %copy-start = (bf16[1024,1024]{1,0:T(8,128)(2,1)S(1)}, bf16[1024,1024]{1,0:T(8,128)(2,1)}, u32[]{:S(2)}) copy-start(bf16[1024,1024]{1,0:T(8,128)(2,1)} %param.18) | copy-start | bytes 6291460
  7.2 60.6 %all-gather.5.cloned.1.call-start = ((), (), s32[]{:S(2)}) async-start(), calls=%async_computation.3 | async-start | bytes 2367488 | tf_op jit(solution)/shard_map/all_gather | solution.py:12
  10.5 124.0 %all-gather.3.cloned.1.call-start = ((), (), s32[]{:S(2)}) async-start(), calls=%async_computation.2 | async-start | bytes 4456448 | tf_op jit(solution)/shard_map/all_gather | solution.py:22
  12.3 384.0 %reduce-scatter.2.cloned.1.call-start = ((), (), s32[]{:S(2)}) async-start(), calls=%async_computation.4 | async-start | bytes 4456448 | tf_op jit(solution)/shard_map/reduce_scatter | solution.py:125
  156.2 1.3 copy-start.1
  158.4 3.9 copy-start.2
  174.3 1.3 copy-start.1
  176.5 3.9 copy-start.2
  192.4 1.3 copy-start.1
  194.7 3.8 copy-start.2
  210.6 1.3 copy-start.1
  212.8 3.9 copy-start.2
  228.7 1.3 copy-start.1
  230.9 3.8 copy-start.2
  246.8 1.3 copy-start.1
  249.0 3.8 copy-start.2
  264.9 1.3 copy-start.1
  267.2 3.9 copy-start.2
  283.1 1.3 copy-start.1
  285.3 3.9 copy-start.2
  290.8 4.7 %copy-start.4 = (f32[1024,1024]{0,1:T(8,128)S(1)}, f32[1024,1024]{0,1:T(8,128)}, u32[]{:S(2)}) copy-start(f32[1024,1024]{0,1:T(8,128)} %get-tuple-element.174) | copy-start | bytes 12582916
  295.5 2.4 copy-start.3
  295.5 2.9 copy-start.5
Sparse Core Ops, SparseCore 0:
  10.8 56.9 all-gather.4
  69.6 64.9 all-gather.2
  305.3 78.8 reduce-scatter.1
where the time goes:
time: 406 us; the launch traced here: 405 us
  waiting for transfers between devices  118 us (29%)
  matrix products  102 us (25%)
  blocking collectives  84.1 us (21%)
  local copies, waits for them, and re-layouts  79.9 us (20%)
  between operations  13.8 us (3%)
  other arithmetic  5.25 us (1%)
    all_to_all x1, blocking collectives, summed_on_arrival(): lax.all_to_all(pieces, axis, split_axis=0, concat_axis=0, tiled=True)  84.1 us
    all_gather x1, waiting for transfers between devices, in_one_piece(): whole, at, outs = (lax.all_gather(both, axis, axis=dim, tiled=True), 0, [])  62.5 us
    all_gather x1, waiting for transfers between devices, turned_gather(): whole, at, outs = (lax.all_gather(both, axis, axis=0, tiled=True), 0, [])  55.4 us
    dynamic_slice x64, local copies, waits for them, and re-layouts, columns(): lax.dynamic_slice_in_dim(source, column, pair_width, 1)  34.3 us
    dot_general x8, matrix products, head_pair(): jnp.einsum('qhd,khd->hqk', grads_out, values_pair, preferred_element_type...  26.8 us
    dot_general x8, matrix products, head_pair(): jnp.einsum('hqk,qhd->khd', probs_b, grads_out, preferred_element_type=jnp...  24.7 us
    dot_general x8, matrix products, head_pair(): jnp.einsum('qhd,khd->hqk', queries, keys_pair, preferred_element_type=jnp...  21.7 us
    dot_general x3, matrix products, project(): lax.dot_general(upper, weights, contract, preferred_element_type=jnp.floa...  11.4 us
  transfers between devices with their start and end apart: 3, of which 2 were waited for; matrix products, arithmetic and copies ran while one was open for 3% of the time, Pallas kernels for 0%

commit v1 on v0

v1 whole, which is shorter than its diff:
```python
import jax
import jax.numpy as jnp
from jax import lax
from jax.experimental import pallas as pl
from jax.experimental.pallas import tpu as pltpu
from jax.sharding import PartitionSpec as P

NX, NY, NZ, NC = 4, 4, 8, 2
PAIRS = NX * NC
LANES = 128
Q_OWN, K_OWN = 32, 64
Q_PART, K_PART = Q_OWN * PAIRS, K_OWN * PAIRS
Q_ALL, K_ALL = Q_PART * NZ, K_PART * NY
TQ, TK = 512, 1024
BF, F32 = jnp.bfloat16, jnp.float32
NT = (((1,), (1,)), ((), ()))
NN = (((1,), (0,)), ((), ()))
TN = (((0,), (0,)), ((), ()))
OTHERS = [(dx, dc) for dx in range(NX) for dc in range(NC) if dx or dc]


def dot(a, b, dims):
    return lax.dot_general(a, b, dims, preferred_element_type=F32)


def rows(start, size):
    return pl.ds(pl.multiple_of(start, size), size)


def kernel(
    q_hbm, k_hbm, v_hbm, g_hbm, norm, delta, wq_hbm, wk_hbm, wv_hbm,
    out_q, out_kv,
    q, g, k, v, aux_out, aux_in, aux,
    qm, gm, an, ad, kt, dqt, dk, dv,
    send_q, send_kv, got_q, got_kv, sum_q, sum_kv, full_q, full_k, full_v,
    wq, wk, wv,
    a_send, a_recv, own_sem, w_sem, z_send, z_recv, y_send, y_recv,
    rq_send, rq_recv, rkv_send, rkv_recv, b_send, b_recv, bown_sem,
):
    pb, ka = lax.axis_index("pb"), lax.axis_index("ka")
    z, y, c = pb % NZ, (ka // NC) % NY, ka % NC
    x = (ka // (NC * NY)) * 2 + pb // NZ
    me = x * NC + c

    def at(x, y, z, c):
        return {"pb": (x % 2) * NZ + z, "ka": (x // 2) * (NY * NC) + y * NC + c}

    def side(dx, dc):
        return at((x + dx) % NX, y, z, (c + dc) % NC)

    def up_z(dz):
        return at(x, y, (z + dz) % NZ, c)

    def up_y(dy):
        return at(x, (y + dy) % NY, z, c)

    def remote(src, dst, send, recv, device):
        return pltpu.make_async_remote_copy(
            src_ref=src, dst_ref=dst, send_sem=send, recv_sem=recv,
            device_id=device, device_id_type=pl.DeviceIdType.MESH,
        )

    peers = [side(dx, dc) for dx, dc in OTHERS]
    peers += [up_z(dz) for dz in range(1, NZ)] + [up_y(dy) for dy in range(1, NY)]
    barrier = pltpu.get_barrier_semaphore()
    for peer in peers:
        pl.semaphore_signal(barrier, inc=1, device_id=peer, device_id_type=pl.DeviceIdType.MESH)
    pl.semaphore_wait(barrier, len(peers))

    my_q = rows(z * Q_PART + me * Q_OWN, Q_OWN)
    my_k = rows(y * K_PART + me * K_OWN, K_OWN)
    sends = []
    for dx, dc in OTHERS:
        j = dx * NC + dc
        cols = rows(((x + dx) % NX * NC + (c + dc) % NC) * LANES, LANES)
        for i, (src, dst, at_rows) in enumerate(
            [(q_hbm, q, my_q), (g_hbm, g, my_q), (k_hbm, k, my_k), (v_hbm, v, my_k)]
        ):
            copy = remote(
                src.at[:, cols], dst.at[at_rows, :], a_send.at[i, j], a_recv.at[i, j], side(dx, dc)
            )
            copy.start()
            sends.append(copy)
    cols = rows(me * LANES, LANES)
    own = []
    for i, (src, dst, at_rows) in enumerate(
        [(q_hbm, q, my_q), (g_hbm, g, my_q), (k_hbm, k, my_k), (v_hbm, v, my_k)]
    ):
        copy = pltpu.make_async_copy(src.at[:, cols], dst.at[at_rows, :], own_sem.at[i])
        copy.start()
        own.append(copy)
    row = lax.broadcasted_iota(jnp.int32, (NX * NC * 2, PAIRS * LANES), 0)
    lane = lax.broadcasted_iota(jnp.int32, (NX * NC * 2, PAIRS * LANES), 1)
    same_pair = lane // LANES == row // 2
    pick = lambda first: jnp.where(
        jnp.logical_and(same_pair, lane % LANES == 4 * me + first + row % 2), -1.0, 0.0
    ).astype(BF)
    aux_out[...] = (dot(norm[...], pick(0), TN) + dot(delta[...], pick(2), TN)).astype(BF)
    for dx, dc in OTHERS:
        j = dx * NC + dc
        cols = rows(((x + dx) % NX * NC + (c + dc) % NC) * LANES, LANES)
        copy = remote(
            aux_out.at[:, cols], aux_in.at[j], a_send.at[4, j], a_recv.at[4, j], side(dx, dc)
        )
        copy.start()
        sends.append(copy)
    weights = []
    for i, (src, dst) in enumerate([(wq_hbm, wq), (wk_hbm, wk), (wv_hbm, wv)]):
        copy = pltpu.make_async_copy(src, dst, w_sem.at[i])
        copy.start()
        weights.append(copy)
    aux_sum = aux_out[:, rows(me * LANES, LANES)].astype(F32)
    for copy in own:
        copy.wait()
    for copy in sends:
        copy.wait()
    for dx, dc in OTHERS:
        aux_sum += aux_in[dx * NC + dc].astype(F32)
    aux[z] = aux_sum.astype(BF)

    def pass_on(step):
        moves = []
        if step <= NZ // 2:
            right, left = (z - step + 1 + NZ) % NZ, (z + step - 1) % NZ
            half = step == NZ // 2
            for i, buf in enumerate([q, g]):
                for d, (origin, to) in enumerate([(right, up_z(1)), (left, up_z(NZ - 1))]):
                    if half and i != d:
                        continue
                    part = buf.at[rows(origin * Q_PART, Q_PART), :]
                    moves.append(remote(
                        part, part, z_send.at[i, d, step - 1], z_recv.at[i, d, step - 1], to
                    ))
            for d, (origin, to) in enumerate([(right, up_z(1)), (left, up_z(NZ - 1))]):
                if half and d:
                    continue
                moves.append(remote(
                    aux.at[origin], aux.at[origin],
                    z_send.at[2, d, step - 1], z_recv.at[2, d, step - 1], to,
                ))
        if step <= NY // 2:
            right, left = (y - step + 1 + NY) % NY, (y + step - 1) % NY
            half = step == NY // 2
            for i, buf in enumerate([k, v]):
                for d, (origin, to) in enumerate([(right, up_y(1)), (left, up_y(NY - 1))]):
                    if half and i != d:
                        continue
                    part = buf.at[rows(origin * K_PART, K_PART), :]
                    moves.append(remote(
                        part, part, y_send.at[i, d, step - 1], y_recv.at[i, d, step - 1], to
                    ))
        return moves

    for step in range(1, NZ // 2 + 1):
        moves = pass_on(step)
        for copy in moves:
            copy.start()
        for copy in moves:
            copy.wait()

    lane = lax.broadcasted_iota(jnp.int32, (Q_PART, LANES), 1)
    row = lax.broadcasted_iota(jnp.int32, (Q_PART, LANES), 0)

    def prepare_q(part, _):
        at_rows = rows(part * Q_PART, Q_PART)
        queries = q[at_rows, :].astype(F32) * 0.125
        grads = g[at_rows, :].astype(F32)
        columns = jnp.concatenate([aux[part].astype(F32)] * PAIRS, axis=0)
        mine = lane // 4 == row // Q_OWN
        for h in range(2):
            head = lane // 64 == h
            qm[h, at_rows, :] = jnp.where(head, queries, 0.0).astype(BF)
            gm[h, at_rows, :] = jnp.where(head, grads, 0.0).astype(BF)
            for dst, first in [(an, 0), (ad, 2)]:
                keep = jnp.logical_and(mine, lane % 4 == first + h)
                dst[h, at_rows, :] = jnp.where(keep, columns, 0.0).astype(BF)
        return 0

    lax.fori_loop(0, NZ, prepare_q, 0)

    def prepare_k(part, _):
        at_rows = rows(part * K_PART, K_PART)
        kt[:, at_rows] = (k[at_rows, :].astype(F32) * 0.125).T.astype(BF)
        return 0

    lax.fori_loop(0, NY, prepare_k, 0)
    dk[...] = jnp.zeros_like(dk)
    dv[...] = jnp.zeros_like(dv)
    dqt[...] = jnp.zeros_like(dqt)
    ones = jnp.ones((TK, LANES), BF)

    def tile(i, _):
        at_q, at_k = rows(i // (K_ALL // TK) * TQ, TQ), rows(i % (K_ALL // TK) * TK, TK)
        keys = jnp.concatenate([k[at_k, :], ones], axis=1)
        values = jnp.concatenate([v[at_k, :], ones], axis=1)
        grad_v = grad_k = None
        for h in range(2):
            scores = dot(keys, jnp.concatenate([qm[h, at_q, :], an[h, at_q, :]], axis=1), NT)
            grads = dot(values, jnp.concatenate([gm[h, at_q, :], ad[h, at_q, :]], axis=1), NT)
            probs = jnp.exp(scores)
            grad_scores = (probs * grads).astype(BF)
            part_v = dot(probs.astype(BF), gm[h, at_q, :], NN)
            part_k = dot(grad_scores, qm[h, at_q, :], NN)
            grad_v = part_v if grad_v is None else grad_v + part_v
            grad_k = part_k if grad_k is None else grad_k + part_k
            head = pl.ds(h * 64, 64)
            dqt[head, at_q] += dot(kt[head, at_k], grad_scores, NN)
        dv[at_k, :] += grad_v
        dk[at_k, :] += grad_k
        return 0

    lax.fori_loop(0, (Q_ALL // TQ) * (K_ALL // TK), tile, 0)

    def pack_q(part, _):
        at_rows = rows(part * Q_PART, Q_PART)
        send_q[at_rows, :] = dqt[:, at_rows].T.astype(BF)
        return 0

    lax.fori_loop(0, NZ, pack_q, 0)
    send_kv[:, :LANES] = dk[...].astype(BF)
    send_kv[:, LANES:] = dv[...].astype(BF)
    moves = []
    for dy in range(1, NY):
        to = (y + dy) % NY
        moves.append(remote(
            send_kv.at[rows(to * K_PART, K_PART), :], got_kv.at[dy - 1],
            rkv_send.at[dy - 1], rkv_recv.at[dy - 1], up_y(dy),
        ))
    for dz in range(1, NZ):
        to = (z + dz) % NZ
        moves.append(remote(
            send_q.at[rows(to * Q_PART, Q_PART), :], got_q.at[dz - 1],
            rq_send.at[dz - 1], rq_recv.at[dz - 1], up_z(dz),
        ))
    for copy in moves:
        copy.start()
    for copy in moves:
        copy.wait()
    total = send_q[rows(z * Q_PART, Q_PART), :].astype(F32)
    for i in range(NZ - 1):
        total += got_q[i].astype(F32)
    sum_q[...] = total.astype(BF)
    total = send_kv[rows(y * K_PART, K_PART), :].astype(F32)
    for i in range(NY - 1):
        total += got_kv[i].astype(F32)
    sum_kv[...] = total.astype(BF)

    cols = rows(me * LANES, LANES)
    moves = []
    for dx, dc in OTHERS:
        j = dx * NC + dc
        to = (x + dx) % NX * NC + (c + dc) % NC
        at_q, at_k = rows(to * Q_OWN, Q_OWN), rows(to * K_OWN, K_OWN)
        for i, (src, dst) in enumerate([
            (sum_q.at[at_q, :], full_q),
            (sum_kv.at[at_k, pl.ds(0, LANES)], full_k),
            (sum_kv.at[at_k, pl.ds(LANES, LANES)], full_v),
        ]):
            moves.append(remote(
                src, dst.at[:, cols], b_send.at[i, j], b_recv.at[i, j], side(dx, dc)
            ))
    at_q, at_k = rows(me * Q_OWN, Q_OWN), rows(me * K_OWN, K_OWN)
    for i, (src, dst) in enumerate([
        (sum_q.at[at_q, :], full_q),
        (sum_kv.at[at_k, pl.ds(0, LANES)], full_k),
        (sum_kv.at[at_k, pl.ds(LANES, LANES)], full_v),
    ]):
        moves.append(pltpu.make_async_copy(src, dst.at[:, cols], bown_sem.at[i]))
    for copy in moves:
        copy.start()
    for copy in weights:
        copy.wait()
    for copy in moves:
        copy.wait()
    out_q[...] = dot(full_q[...], wq[...], NT).astype(BF)
    out_kv[...] = (dot(full_k[...], wk[...], NT) + dot(full_v[...], wv[...], NT)).astype(BF)


def local(query_saved, key_saved, value_saved, out_grad, log_norm, row_delta, wq, wk, wv):
    width = query_saved.shape[1]
    hbm, vmem = pl.BlockSpec(memory_space=pl.ANY), pl.BlockSpec(memory_space=pltpu.VMEM)
    dma = pltpu.SemaphoreType.DMA
    return pl.pallas_call(
        kernel,
        out_shape=(
            jax.ShapeDtypeStruct((Q_OWN, width), BF),
            jax.ShapeDtypeStruct((K_OWN, width), BF),
        ),
        in_specs=[hbm] * 4 + [vmem] * 2 + [hbm] * 3,
        out_specs=(vmem, vmem),
        scratch_shapes=[
            pltpu.VMEM((Q_ALL, LANES), BF), pltpu.VMEM((Q_ALL, LANES), BF),
            pltpu.VMEM((K_ALL, LANES), BF), pltpu.VMEM((K_ALL, LANES), BF),
            pltpu.VMEM((Q_OWN, width), BF), pltpu.VMEM((PAIRS, Q_OWN, LANES), BF),
            pltpu.VMEM((NZ, Q_OWN, LANES), BF),
            *[pltpu.VMEM((2, Q_ALL, LANES), BF)] * 4,
            pltpu.VMEM((LANES, K_ALL), BF), pltpu.VMEM((LANES, Q_ALL), F32),
            pltpu.VMEM((K_ALL, LANES), F32), pltpu.VMEM((K_ALL, LANES), F32),
            pltpu.VMEM((Q_ALL, LANES), BF), pltpu.VMEM((K_ALL, 2 * LANES), BF),
            pltpu.VMEM((NZ - 1, Q_PART, LANES), BF), pltpu.VMEM((NY - 1, K_PART, 2 * LANES), BF),
            pltpu.VMEM((Q_PART, LANES), BF), pltpu.VMEM((K_PART, 2 * LANES), BF),
            pltpu.VMEM((Q_OWN, width), BF), pltpu.VMEM((K_OWN, width), BF),
            pltpu.VMEM((K_OWN, width), BF),
            *[pltpu.VMEM((width, width), BF)] * 3,
            dma((5, PAIRS)), dma((5, PAIRS)), dma((4,)), dma((3,)),
            dma((3, 2, NZ // 2)), dma((3, 2, NZ // 2)), dma((2, 2, NY // 2)), dma((2, 2, NY // 2)),
            dma((NZ - 1,)), dma((NZ - 1,)), dma((NY - 1,)), dma((NY - 1,)),
            dma((3, PAIRS)), dma((3, PAIRS)), dma((3,)),
        ],
        compiler_params=pltpu.CompilerParams(
            collective_id=0, has_side_effects=True, vmem_limit_bytes=60 * 2**20
        ),
        name="attention_backward",
    )(query_saved, key_saved, value_saved, out_grad, log_norm, row_delta, wq, wk, wv)


def solution(mesh):
    in_specs = (
        P(("pb", "ka"), None),
        P(("ka", "pb"), None),
        P(("ka", "pb"), None),
        P(("pb", "ka"), None),
        P(None, ("pb", "ka")),
        P(None, ("pb", "ka")),
        P(),
        P(),
        P(),
    )
    out_specs = (P(("pb", "ka"), None), P(("ka", "pb"), None))
    return jax.shard_map(local, mesh=mesh, in_specs=in_specs, out_specs=out_specs, check_vma=False)
```

time: 406 us -> 89.2 us (0.22)
  waiting for transfers between devices: 118 us -> 0 us
  matrix products: 102 us -> 0 us
  Pallas kernels: 0 us -> 85.3 us
  blocking collectives: 84.1 us -> 0 us
  local copies, waits for them, and re-layouts: 79.9 us -> 3.04 us
  between operations: 13.8 us -> 0.64 us
  other arithmetic: 5.25 us -> 0 us
    all_gather x2 -> x0, waiting for transfers between devices: 118 us -> none  [the longest x1 62.5 us: in_one_piece(): whole, at, outs = (lax.all_gather(both, axis, axis=dim, tiled=True), 0, [])]
    dot_general x46 -> x0, matrix products: 102 us -> none  [the longest x8 26.8 us: head_pair(): jnp.einsum('qhd,khd->hqk', grads_out, values_pair, preferred_element_type...]
    pallas_call x0 -> x1, Pallas kernels: none -> 85.3 us  [local(): pl.pallas_call(kernel, out_shape=(jax.ShapeDtypeStruct((Q_OWN, width), BF...]
    all_to_all x1 -> x0, blocking collectives: 84.1 us -> none  [summed_on_arrival(): lax.all_to_all(pieces, axis, split_axis=0, concat_axis=0, tiled=True)]
    dynamic_slice x64 -> x0, local copies, waits for them, and re-layouts: 34.3 us -> none  [columns(): lax.dynamic_slice_in_dim(source, column, pair_width, 1)]
    dynamic_update_slice x24 -> x0, local copies, waits for them, and re-layouts: 15.8 us -> none  [the longest x8 8.73 us: head_pair(): lax.dynamic_update_slice_in_dim(grad_value, value_part.reshape(key_rows,...]
    while x34 -> x0, local copies, waits for them, and re-layouts: 10.7 us -> none
    slice x2 -> x0, local copies, waits for them, and re-layouts: 7.66 us -> none  [the longest x1 4.59 us: in_one_piece(): outs.append(lax.slice_in_dim(whole, at, at + a.shape[along], axis=along))]
  transfers between devices with their start and end apart: 3 -> 0, of which waited for: 2 -> 0; matrix products, arithmetic and copies ran while one was open for 3% -> 0% of each run, Pallas kernels for 0% -> 0%
where the time goes in v1:
time: 89.2 us; the launch traced here: 89 us
  Pallas kernels  85.3 us (96%)
  local copies, waits for them, and re-layouts  3.04 us (3%)
    pallas_call x1, Pallas kernels, local(): pl.pallas_call(kernel, out_shape=(jax.ShapeDtypeStruct((Q_OWN, width), BF...  85.3 us
    unnamed x2, local copies, waits for them, and re-layouts  3.04 us

profile of v1, /device:TPU:1, one launch (start us, length us, event | category | flops | bytes accessed | tf_op | source)
XLA Modules:
  0.0 89.0 jit_solution(674029149760406883)
XLA Ops:
  0.6 85.3 %attention_backward.1 = (bf16[32,1024]{1,0:T(8,128)(2,1)}, bf16[64,1024]{1,0:T(8,128)(2,1)}) custom-call(bf16[32,1024]{1,0:T(8,128)(2,1)} %q_hbm.1, bf16[64,1024]{1,0:T(8,128)(2,1)} %k_hbm.1, bf16[64,1024]{1,0:T(8,128)(2,1)} %v_hbm.1, bf16[32,1024]{1,0:T(8,128)(2,1)} %g_hbm.1, bf16[16,32]{1,0:T(8,128)(2,1)} %norm.1, bf16[16,32]{1,0:T(8,128)(2,1)} %delta.1, ...), custom_call_target="tpu_custom_call" | custom-call | tf_op jit(solution)/shard_map/attention_backward/pallas_call | solution.py:283
  85.9 1.5 %copy.13 = bf16[32,1024]{1,0:T(8,128)(2,1)} copy(bf16[32,1024]{1,0:T(8,128)(2,1)} %get-tuple-element.4) | data formatting | bytes 131072
  87.4 1.6 %copy.14 = bf16[64,1024]{1,0:T(8,128)(2,1)} copy(bf16[64,1024]{1,0:T(8,128)(2,1)} %get-tuple-element.5) | data formatting | bytes 262144

commit v2 on v1

v2 whole, which is shorter than its diff:
```python
import jax
import jax.numpy as jnp
from jax import lax
from jax.experimental import pallas as pl
from jax.experimental.pallas import tpu as pltpu
from jax.sharding import PartitionSpec as P

NX, NY, NZ, NC = 4, 4, 8, 2
PAIRS = NX * NC
LANES = 128
Q_OWN, K_OWN = 32, 64
Q_PART, K_PART = Q_OWN * PAIRS, K_OWN * PAIRS
Q_ALL, K_ALL = Q_PART * NZ, K_PART * NY
BF, F32 = jnp.bfloat16, jnp.float32
NT = (((1,), (1,)), ((), ()))
NN = (((1,), (0,)), ((), ()))
TN = (((0,), (0,)), ((), ()))
MESH = pl.DeviceIdType.MESH
OTHERS = [(dx, dc) for dx in range(NX) for dc in range(NC) if dx or dc]


def dot(a, b, dims):
    return lax.dot_general(a, b, dims, preferred_element_type=F32)


def rows(start, size):
    return pl.ds(pl.multiple_of(start, size), size)


def kernel(
    q_hbm, k_hbm, v_hbm, g_hbm, norm, delta, wq_hbm, wk_hbm, wv_hbm,
    out_q, out_kv,
    q, g, k, v, aux_out, aux_in, aux,
    qm, gm, qr, an, ad, kt, dqt, acc,
    send_q, send_kv, got_q, got_kv, sum_q, sum_kv, full_q, full_k, full_v,
    wq, wk, wv,
    a_send, a_recv, own_sem, w_sem, z1_send, z1_recv, y1_send, y1_recv,
    z_send, z_recv, y_send, y_recv,
    rq_send, rq_recv, rkv_send, rkv_recv, b_send, b_recv, bown_sem,
):
    pb, ka = lax.axis_index("pb"), lax.axis_index("ka")
    z, y, c = pb % NZ, (ka // NC) % NY, ka % NC
    x = (ka // (NC * NY)) * 2 + pb // NZ
    me = x * NC + c

    def at(x, y, z, c):
        return {"pb": (x % 2) * NZ + z, "ka": (x // 2) * (NY * NC) + y * NC + c}

    def side(dx, dc):
        return at((x + dx) % NX, y, z, (c + dc) % NC)

    def ring(here, place, size):
        return (here + (place + 1) // 2 * (place % 2 * 2 - 1) + size) % size

    def z_at(place):
        return ring(z, place, NZ)

    def y_at(place):
        return ring(y, place, NY)

    def to_z(z):
        return at(x, y, z, c)

    def to_y(y):
        return at(x, y, z, c)

    def remote(src, dst, send, recv, device):
        return pltpu.make_async_remote_copy(
            src_ref=src, dst_ref=dst, send_sem=send, recv_sem=recv,
            device_id=device, device_id_type=MESH,
        )

    peers = [side(dx, dc) for dx, dc in OTHERS]
    peers += [to_z(z_at(i)) for i in range(1, NZ)] + [to_y(y_at(i)) for i in range(1, NY)]
    barrier = pltpu.get_barrier_semaphore()
    for peer in peers:
        pl.semaphore_signal(barrier, inc=1, device_id=peer, device_id_type=MESH)

    my_q = rows(z * Q_PART + me * Q_OWN, Q_OWN)
    my_k = rows(y * K_PART + me * K_OWN, K_OWN)
    exchanged = [(q_hbm, q, my_q), (g_hbm, g, my_q), (k_hbm, k, my_k), (v_hbm, v, my_k)]
    mine = rows(me * LANES, LANES)
    own = [
        pltpu.make_async_copy(src.at[:, mine], dst.at[at_rows, :], own_sem.at[i])
        for i, (src, dst, at_rows) in enumerate(exchanged)
    ]
    for copy in own:
        copy.start()
    row = lax.broadcasted_iota(jnp.int32, (NX * NC * 2, PAIRS * LANES), 0)
    lane = lax.broadcasted_iota(jnp.int32, (NX * NC * 2, PAIRS * LANES), 1)
    same_pair = lane // LANES == row // 2
    pick = lambda first: jnp.where(
        jnp.logical_and(same_pair, lane % LANES == 4 * me + first + row % 2), -1.0, 0.0
    ).astype(BF)
    aux_out[...] = (dot(norm[...], pick(0), TN) + dot(delta[...], pick(2), TN)).astype(BF)
    acc[...] = jnp.zeros_like(acc)
    dqt[...] = jnp.zeros_like(dqt)
    pl.semaphore_wait(barrier, len(peers))

    sent = []
    arrivals = {}
    for dx in (1, 3, 2, 0):
        arrivals[dx] = []
        for dc in range(NC):
            if not (dx or dc):
                continue
            j = dx * NC + dc
            cols = rows(((x + dx) % NX * NC + (c + dc) % NC) * LANES, LANES)
            moves = [
                remote(src.at[:, cols], dst.at[at_rows, :], a_send.at[i, j], a_recv.at[i, j], side(dx, dc))
                for i, (src, dst, at_rows) in enumerate(exchanged)
            ]
            moves.append(remote(
                aux_out.at[:, cols], aux_in.at[j], a_send.at[4, j], a_recv.at[4, j], side(dx, dc)
            ))
            for copy in moves:
                copy.start()
            sent += moves
            arrivals[dx] += moves
    weights = [
        pltpu.make_async_copy(src, dst, w_sem.at[i])
        for i, (src, dst) in enumerate([(wq_hbm, wq), (wk_hbm, wk), (wv_hbm, wv)])
    ]

    z_ways = [to_z(z_at(1)), to_z(z_at(2))]
    y_ways = [to_y(y_at(1)), to_y(y_at(2))]
    first_z, first_y = [], []
    for copy in own:
        copy.wait()
    for dx in (0, 1, 3, 2):
        for copy in arrivals[dx]:
            copy.wait_recv()
        from_x = (x - dx + NX) % NX
        at_q = rows(z * Q_PART + from_x * NC * Q_OWN, NC * Q_OWN)
        at_k = rows(y * K_PART + from_x * NC * K_OWN, NC * K_OWN)
        for d in range(2):
            for i, buf in enumerate([q, g]):
                part = buf.at[at_q, :]
                first_z.append(remote(part, part, z1_send.at[i, d, dx], z1_recv.at[i, d, dx], z_ways[d]))
                first_z[-1].start()
            for i, buf in enumerate([k, v]):
                part = buf.at[at_k, :]
                first_y.append(remote(part, part, y1_send.at[i, d, dx], y1_recv.at[i, d, dx], y_ways[d]))
                first_y[-1].start()
    aux_sum = aux_out[:, mine].astype(F32)
    for dx, dc in OTHERS:
        aux_sum += aux_in[dx * NC + dc].astype(F32)
    aux[z] = aux_sum.astype(BF)

    def hop_z(step):
        moves = []
        origins = [(z - step + 1 + NZ) % NZ, (z + step - 1) % NZ]
        for i, buf in enumerate([q, g, aux]):
            if step == 1 and i < 2:
                continue
            for d in range(2):
                if step == NZ // 2 and d != i % 2:
                    continue
                part = aux.at[origins[d]] if i == 2 else buf.at[rows(origins[d] * Q_PART, Q_PART), :]
                moves.append(remote(
                    part, part, z_send.at[i, d, step - 1], z_recv.at[i, d, step - 1], z_ways[d]
                ))
        return moves

    def hop_y():
        moves = []
        for i, (buf, origin) in enumerate([(k, (y - 1 + NY) % NY), (v, (y + 1) % NY)]):
            part = buf.at[rows(origin * K_PART, K_PART), :]
            moves.append(remote(part, part, y_send.at[i], y_recv.at[i], y_ways[i]))
        return moves

    def start(moves):
        for copy in moves:
            copy.start()
        return moves

    def arrive(moves):
        for copy in moves:
            copy.wait_recv()

    aux_hops = start(hop_z(1))
    for copy in weights:
        copy.start()

    lane = lax.broadcasted_iota(jnp.int32, (Q_PART, LANES), 1)
    row = lax.broadcasted_iota(jnp.int32, (Q_PART, LANES), 0)
    ones = jnp.ones((K_PART, LANES), BF)

    def prepare_q(place):
        part = z_at(place)
        at_rows = rows(part * Q_PART, Q_PART)
        queries = q[at_rows, :].astype(F32) * 0.125
        turned = pltpu.roll(queries, LANES // 2, 1)
        grads = g[at_rows, :].astype(F32)
        columns = jnp.concatenate([aux[part].astype(F32)] * PAIRS, axis=0)
        source = lane // 4 == row // Q_OWN
        for h in range(2):
            head = lane // 64 == h
            qm[h, at_rows, :] = jnp.where(head, queries, 0.0).astype(BF)
            qr[h, at_rows, :] = jnp.where(head, 0.0, turned).astype(BF)
            gm[h, at_rows, :] = jnp.where(head, grads, 0.0).astype(BF)
            for dst, first in [(an, 0), (ad, 2)]:
                keep = jnp.logical_and(source, lane % 4 == first + h)
                dst[h, at_rows, :] = jnp.where(keep, columns, 0.0).astype(BF)

    def prepare_k(place):
        at_rows = rows(y_at(place) * K_PART, K_PART)
        kt[:, at_rows] = (k[at_rows, :].astype(F32) * 0.125).T.astype(BF)

    def attend(items):
        made = []
        for h, qp, kp in items:
            at_q, at_k = rows(z_at(qp) * Q_PART, Q_PART), rows(y_at(kp) * K_PART, K_PART)
            keys = jnp.concatenate([k[at_k, :], ones], axis=1)
            values = jnp.concatenate([v[at_k, :], ones], axis=1)
            scores = dot(keys, jnp.concatenate([qm[h, at_q, :], an[h, at_q, :]], axis=1), NT)
            grads = dot(values, jnp.concatenate([gm[h, at_q, :], ad[h, at_q, :]], axis=1), NT)
            probs = jnp.exp(scores)
            made.append((h, qp, kp, at_q, at_k, probs.astype(BF), (probs * grads).astype(BF)))
        by_keys, by_queries = {}, {}
        for item in made:
            by_keys.setdefault((item[0], str(item[2])), []).append(item)
            by_queries.setdefault((item[0], str(item[1])), []).append(item)
        for group in by_keys.values():
            h, at_k = group[0][0], group[0][4]
            left = jnp.concatenate([part for item in group for part in item[5:7]], axis=1)
            right = jnp.concatenate(
                [part for item in group for part in (gm[h, item[3], :], qr[h, item[3], :])], axis=0
            )
            acc[h, at_k, :] += dot(left, right, NN)
        for group in by_queries.values():
            h, at_q = group[0][0], group[0][3]
            head = pl.ds(h * 64, 64)
            left = jnp.concatenate([kt[head, item[4]] for item in group], axis=1)
            right = jnp.concatenate([item[6] for item in group], axis=0)
            dqt[head, at_q] += dot(left, right, NN)

    def loop(count, body):
        def step(i, _):
            body(i)
            return 0

        lax.fori_loop(0, count, step, 0)

    def both(qp, kp):
        attend([(0, qp, kp), (1, qp, kp)])

    def give_q(h, place):
        at_rows = rows(z_at(place) * Q_PART, Q_PART)
        return remote(
            send_q.at[h, :, at_rows], got_q.at[h, place - 1],
            rq_send.at[h, place - 1], rq_recv.at[h, place - 1], to_z(z_at(place)),
        )

    def give_k(h, place):
        at_rows = rows(y_at(place) * K_PART, K_PART)
        return remote(
            send_kv.at[h, at_rows, :], got_kv.at[h, place - 1],
            rkv_send.at[h, place - 1], rkv_recv.at[h, place - 1], to_y(y_at(place)),
        )

    def finish_q(h, place):
        at_rows = rows(z_at(place) * Q_PART, Q_PART)
        send_q[h, :, at_rows] = dqt[pl.ds(h * 64, 64), at_rows].astype(BF)
        give_q(h, place).start()

    def finish_k(h, place):
        at_rows = rows(y_at(place) * K_PART, K_PART)
        send_kv[h, at_rows, :] = acc[h, at_rows, :].astype(BF)
        give_k(h, place).start()

    prepare_q(0)
    prepare_k(0)
    both(0, 0)
    arrive(first_z)
    arrive(aux_hops)
    hops_2 = start(hop_z(2))
    loop(2, lambda i: prepare_q(i + 1))
    loop(2, lambda i: both(i + 1, 0))
    arrive(first_y)
    across = start(hop_y())
    loop(2, lambda i: prepare_k(i + 1))
    loop(3, lambda i: both(i, 1))
    arrive(hops_2)
    hops_3 = start(hop_z(3))
    loop(3, lambda i: both(i, 2))
    loop(2, lambda i: prepare_q(i + 3))
    loop(3, lambda i: attend([(0, 3, i), (0, 4, i)]))
    arrive(across)
    prepare_k(3)
    loop(3, lambda i: both(i, 3))
    arrive(hops_3)
    hops_4 = start(hop_z(4))
    loop(2, lambda i: both(i + 3, 3))
    loop(2, lambda i: prepare_q(i + 5))
    arrive(hops_4)
    prepare_q(7)

    def last_of_0(i):
        place = 3 - i
        attend([(0, 5, place), (0, 6, place), (0, 7, place)])

        @pl.when(place > 0)
        def _():
            finish_k(0, place)

    loop(4, last_of_0)
    loop(7, lambda i: finish_q(0, 7 - i))
    attend([(1, 5, 3), (1, 6, 3), (1, 7, 3)])
    finish_k(1, 3)
    loop(2, lambda i: finish_q(1, 2 - i))
    attend([(1, i, 1) for i in range(3, 8)])
    finish_k(1, 1)

    def last_of_1(i):
        place = 7 - i
        attend([(1, place, 2), (1, place, 0)])
        finish_q(1, place)

    loop(5, last_of_1)
    finish_k(1, 2)

    back = []

    def give_back(i, src, dst):
        for dx, dc in OTHERS:
            j = dx * NC + dc
            to = (x + dx) % NX * NC + (c + dc) % NC
            back.append(remote(
                src(to), dst.at[:, mine], b_send.at[i, j], b_recv.at[i, j], side(dx, dc)
            ))
            back[-1].start()
        back.append(pltpu.make_async_copy(src(me), dst.at[:, mine], bown_sem.at[i]))
        back[-1].start()

    at_rows = rows(z * Q_PART, Q_PART)
    halves = []
    for h in range(2):
        total = dqt[pl.ds(h * 64, 64), at_rows]
        for place in range(1, NZ):
            give_q(h, place).wait_recv()
            total += got_q[h, place - 1].astype(F32)
        halves.append(total)
    sum_q[...] = jnp.concatenate(halves, axis=0).T.astype(BF)
    give_back(0, lambda to: sum_q.at[rows(to * Q_OWN, Q_OWN), :], full_q)
    at_rows = rows(y * K_PART, K_PART)
    halves = []
    for h in range(2):
        total = acc[h, at_rows, :]
        for place in range(1, NY):
            give_k(h, place).wait_recv()
            total += got_kv[h, place - 1].astype(F32)
        halves.append(total)
    lane = lax.broadcasted_iota(jnp.int32, (K_PART, LANES), 1)
    turned = [pltpu.roll(half, LANES // 2, 1) for half in halves]
    sum_kv[0] = jnp.where(lane < 64, turned[0], turned[1]).astype(BF)
    sum_kv[1] = jnp.where(lane < 64, halves[0], halves[1]).astype(BF)
    give_back(1, lambda to: sum_kv.at[0, rows(to * K_OWN, K_OWN), :], full_k)
    give_back(2, lambda to: sum_kv.at[1, rows(to * K_OWN, K_OWN), :], full_v)

    for copy in sent + first_z + first_y + aux_hops + hops_2 + hops_3 + hops_4 + across:
        copy.wait_send()
    for h in range(2):
        for place in range(1, NZ):
            give_q(h, place).wait_send()
        for place in range(1, NY):
            give_k(h, place).wait_send()
    for copy in weights:
        copy.wait()
    for copy in back[:PAIRS]:
        copy.wait()
    out_q[...] = dot(full_q[...], wq[...], NT).astype(BF)
    for copy in back[PAIRS:]:
        copy.wait()
    out_kv[...] = (dot(full_k[...], wk[...], NT) + dot(full_v[...], wv[...], NT)).astype(BF)


def local(query_saved, key_saved, value_saved, out_grad, log_norm, row_delta, wq, wk, wv):
    width = query_saved.shape[1]
    hbm, vmem = pl.BlockSpec(memory_space=pl.ANY), pl.BlockSpec(memory_space=pltpu.VMEM)
    dma = pltpu.SemaphoreType.DMA
    return pl.pallas_call(
        kernel,
        out_shape=(
            jax.ShapeDtypeStruct((Q_OWN, width), BF),
            jax.ShapeDtypeStruct((K_OWN, width), BF),
        ),
        in_specs=[hbm] * 4 + [vmem] * 2 + [hbm] * 3,
        out_specs=(vmem, vmem),
        scratch_shapes=[
            pltpu.VMEM((Q_ALL, LANES), BF), pltpu.VMEM((Q_ALL, LANES), BF),
            pltpu.VMEM((K_ALL, LANES), BF), pltpu.VMEM((K_ALL, LANES), BF),
            pltpu.VMEM((Q_OWN, width), BF), pltpu.VMEM((PAIRS, Q_OWN, LANES), BF),
            pltpu.VMEM((NZ, Q_OWN, LANES), BF),
            *[pltpu.VMEM((2, Q_ALL, LANES), BF)] * 5,
            pltpu.VMEM((LANES, K_ALL), BF), pltpu.VMEM((LANES, Q_ALL), F32),
            pltpu.VMEM((2, K_ALL, LANES), F32),
            pltpu.VMEM((2, 64, Q_ALL), BF), pltpu.VMEM((2, K_ALL, LANES), BF),
            pltpu.VMEM((2, NZ - 1, 64, Q_PART), BF), pltpu.VMEM((2, NY - 1, K_PART, LANES), BF),
            pltpu.VMEM((Q_PART, LANES), BF), pltpu.VMEM((2, K_PART, LANES), BF),
            pltpu.VMEM((Q_OWN, width), BF), pltpu.VMEM((K_OWN, width), BF),
            pltpu.VMEM((K_OWN, width), BF),
            *[pltpu.VMEM((width, width), BF)] * 3,
            dma((5, PAIRS)), dma((5, PAIRS)), dma((4,)), dma((3,)),
            dma((2, 2, NX)), dma((2, 2, NX)), dma((2, 2, NX)), dma((2, 2, NX)),
            dma((3, 2, NZ // 2)), dma((3, 2, NZ // 2)), dma((2,)), dma((2,)),
            dma((2, NZ - 1)), dma((2, NZ - 1)), dma((2, NY - 1)), dma((2, NY - 1)),
            dma((3, PAIRS)), dma((3, PAIRS)), dma((3,)),
        ],
        compiler_params=pltpu.CompilerParams(
            collective_id=0, has_side_effects=True, vmem_limit_bytes=60 * 2**20
        ),
        name="attention_backward",
    )(query_saved, key_saved, value_saved, out_grad, log_norm, row_delta, wq, wk, wv)


def solution(mesh):
    in_specs = (
        P(("pb", "ka"), None),
        P(("ka", "pb"), None),
        P(("ka", "pb"), None),
        P(("pb", "ka"), None),
        P(None, ("pb", "ka")),
        P(None, ("pb", "ka")),
        P(),
        P(),
        P(),
    )
    out_specs = (P(("pb", "ka"), None), P(("ka", "pb"), None))
    return jax.shard_map(local, mesh=mesh, in_specs=in_specs, out_specs=out_specs, check_vma=False)
```

time: 89.2 us -> 68.7 us (0.77)
  Pallas kernels: 85.3 us -> 64.9 us
    pallas_call x1, Pallas kernels: 85.3 us -> 64.9 us  [local(): pl.pallas_call(kernel, out_shape=(jax.ShapeDtypeStruct((Q_OWN, width), BF...]
where the time goes in v2:
time: 68.7 us; the launch traced here: 68.6 us
  Pallas kernels  64.9 us (94%)
  local copies, waits for them, and re-layouts  3.04 us (4%)
    pallas_call x1, Pallas kernels, local(): pl.pallas_call(kernel, out_shape=(jax.ShapeDtypeStruct((Q_OWN, width), BF...  64.9 us
    unnamed x2, local copies, waits for them, and re-layouts  3.04 us

profile of v2, /device:TPU:1, one launch (start us, length us, event | category | flops | bytes accessed | tf_op | source)
XLA Modules:
  0.0 68.6 jit_solution(12333175804069331607)
XLA Ops:
  0.6 64.9 %attention_backward.1 = (bf16[32,1024]{1,0:T(8,128)(2,1)}, bf16[64,1024]{1,0:T(8,128)(2,1)}) custom-call(bf16[32,1024]{1,0:T(8,128)(2,1)} %q_hbm.1, bf16[64,1024]{1,0:T(8,128)(2,1)} %k_hbm.1, bf16[64,1024]{1,0:T(8,128)(2,1)} %v_hbm.1, bf16[32,1024]{1,0:T(8,128)(2,1)} %g_hbm.1, bf16[16,32]{1,0:T(8,128)(2,1)} %norm.1, bf16[16,32]{1,0:T(8,128)(2,1)} %delta.1, ...), custom_call_target="tpu_custom_call" | custom-call | tf_op jit(solution)/shard_map/attention_backward/pallas_call | solution.py:382
  65.5 1.5 %copy.13 = bf16[32,1024]{1,0:T(8,128)(2,1)} copy(bf16[32,1024]{1,0:T(8,128)(2,1)} %get-tuple-element.4) | data formatting | bytes 131072
  67.0 1.6 %copy.14 = bf16[64,1024]{1,0:T(8,128)(2,1)} copy(bf16[64,1024]{1,0:T(8,128)(2,1)} %get-tuple-element.5) | data formatting | bytes 262144

commit v3 on v2

v3 whole, which is shorter than its diff:
```python
import jax
import jax.numpy as jnp
from jax import lax
from jax.experimental import pallas as pl
from jax.experimental.pallas import tpu as pltpu
from jax.sharding import PartitionSpec as P

NX, NY, NZ, NC = 4, 4, 8, 2
PAIRS = NX * NC
LANES = 128
Q_OWN, K_OWN = 32, 64
Q_PART, K_PART = Q_OWN * PAIRS, K_OWN * PAIRS
Q_ALL, K_ALL = Q_PART * NZ, K_PART * NY
BF, F32 = jnp.bfloat16, jnp.float32
NT = (((1,), (1,)), ((), ()))
NN = (((1,), (0,)), ((), ()))
TN = (((0,), (0,)), ((), ()))
MESH = pl.DeviceIdType.MESH
OTHERS = [(dx, dc) for dx in range(NX) for dc in range(NC) if dx or dc]


def dot(a, b, dims):
    return lax.dot_general(a, b, dims, preferred_element_type=F32)


def rows(start, size):
    return pl.ds(pl.multiple_of(start, size), size)


def kernel(
    q_hbm, k_hbm, v_hbm, g_hbm, norm_hbm, delta_hbm, wq_hbm, wk_hbm, wv_hbm,
    out_q, out_kv,
    q, g, k, v, norm, delta, aux_out, aux_in, aux,
    qa, qr, ga, gm, ks, vs, kt, dqt, acc,
    send_q, send_kv, got_q, got_kv, sum_q, sum_kv, full_q, full_kv,
    wq, wk, wv, tally,
    own_sem, w_sem, sent_sem, a_recv, z_recv, y_recv, rq_recv, rkv_recv, b_recv,
):
    pb, ka = lax.axis_index("pb"), lax.axis_index("ka")
    z, y, c = pb % NZ, (ka // NC) % NY, ka % NC
    x = (ka // (NC * NY)) * 2 + pb // NZ
    me = x * NC + c

    def at(x, y, z, c):
        return {"pb": (x % 2) * NZ + z, "ka": (x // 2) * (NY * NC) + y * NC + c}

    def side(dx, dc):
        return at((x + dx) % NX, y, z, (c + dc) % NC)

    def ring(here, place, size):
        return (here + (place + 1) // 2 * (place % 2 * 2 - 1) + size) % size

    def z_at(place):
        return ring(z, place, NZ)

    def y_at(place):
        return ring(y, place, NY)

    def to_z(z):
        return at(x, y, z, c)

    def to_y(y):
        return at(x, y, z, c)

    def remote(src, dst, send, recv, device):
        return pltpu.make_async_remote_copy(
            src_ref=src, dst_ref=dst, send_sem=send, recv_sem=recv,
            device_id=device, device_id_type=MESH,
        )

    def landed(sem, count):
        part = tally.at[pl.ds(0, count), :]
        pltpu.make_async_copy(part, part, sem).wait()

    peers = [side(dx, dc) for dx, dc in OTHERS]
    peers += [to_z(z_at(i)) for i in range(1, NZ)] + [to_y(y_at(i)) for i in range(1, NY)]
    barrier = pltpu.get_barrier_semaphore()
    for peer in peers:
        pl.semaphore_signal(barrier, inc=1, device_id=peer, device_id_type=MESH)

    my_q = rows(z * Q_PART + me * Q_OWN, Q_OWN)
    my_k = rows(y * K_PART + me * K_OWN, K_OWN)
    exchanged = [(q_hbm, q, my_q), (g_hbm, g, my_q), (k_hbm, k, my_k), (v_hbm, v, my_k)]
    mine = rows(me * LANES, LANES)
    own = [
        pltpu.make_async_copy(src.at[:, mine], dst.at[at_rows, :], own_sem.at[i])
        for i, (src, dst, at_rows) in enumerate(exchanged)
    ]
    own += [
        pltpu.make_async_copy(norm_hbm, norm, own_sem.at[4]),
        pltpu.make_async_copy(delta_hbm, delta, own_sem.at[5]),
    ]
    for copy in own:
        copy.start()
    row = lax.broadcasted_iota(jnp.int32, (NX * NC * 2, PAIRS * LANES), 0)
    lane = lax.broadcasted_iota(jnp.int32, (NX * NC * 2, PAIRS * LANES), 1)
    same_pair = lane // LANES == row // 2
    pick = lambda first: jnp.where(
        jnp.logical_and(same_pair, lane % LANES == 4 * me + first + row % 2), -1.0, 0.0
    ).astype(BF)
    for copy in own:
        copy.wait()
    aux_out[...] = (dot(norm[...], pick(0), TN) + dot(delta[...], pick(2), TN)).astype(BF)
    acc[...] = jnp.zeros_like(acc)
    dqt[...] = jnp.zeros_like(dqt)
    pl.semaphore_wait(barrier, len(peers))

    for dx in (0, 1, 3, 2):
        for dc in range(NC):
            if not (dx or dc):
                continue
            j = dx * NC + dc
            cols = rows(((x + dx) % NX * NC + (c + dc) % NC) * LANES, LANES)
            for src, dst, at_rows in exchanged:
                remote(src.at[:, cols], dst.at[at_rows, :], sent_sem.at[0], a_recv.at[dx], side(dx, dc)).start()
            remote(aux_out.at[:, cols], aux_in.at[j], sent_sem.at[0], a_recv.at[dx], side(dx, dc)).start()
    per_peer = 3 * Q_OWN + 2 * K_OWN
    weights = [
        pltpu.make_async_copy(src, dst, w_sem.at[i])
        for i, (src, dst) in enumerate([(wq_hbm, wq), (wk_hbm, wk), (wv_hbm, wv)])
    ]

    z_ways = [to_z(z_at(1)), to_z(z_at(2))]
    y_ways = [to_y(y_at(1)), to_y(y_at(2))]
    for dx in (0, 1, 3, 2):
        landed(a_recv.at[dx], per_peer * (NC if dx else NC - 1))
        from_x = (x - dx + NX) % NX
        at_q = rows(z * Q_PART + from_x * NC * Q_OWN, NC * Q_OWN)
        at_k = rows(y * K_PART + from_x * NC * K_OWN, NC * K_OWN)
        for buf in (k, v):
            for d in range(2):
                part = buf.at[at_k, :]
                remote(part, part, sent_sem.at[1], y_recv.at[0], y_ways[d]).start()
        for buf in (q, g):
            for d in range(2):
                part = buf.at[at_q, :]
                remote(part, part, sent_sem.at[0], z_recv.at[0], z_ways[d]).start()
    aux_sum = aux_out[:, mine].astype(F32)
    for dx, dc in OTHERS:
        aux_sum += aux_in[dx * NC + dc].astype(F32)
    aux[z] = aux_sum.astype(BF)

    def hop_z(step):
        moves = []
        origins = [(z - step + 1 + NZ) % NZ, (z + step - 1) % NZ]
        for i, buf in enumerate([q, g, aux]):
            if step == 1 and i < 2:
                continue
            for d in range(2):
                if step == NZ // 2 and d != i % 2:
                    continue
                part = aux.at[origins[d]] if i == 2 else buf.at[rows(origins[d] * Q_PART, Q_PART), :]
                moves.append(remote(
                    part, part, sent_sem.at[0], z_recv.at[step - 1], z_ways[d]
                ))
        return moves

    def hop_y():
        moves = []
        for i, (buf, origin) in enumerate([(k, (y - 1 + NY) % NY), (v, (y + 1) % NY)]):
            part = buf.at[rows(origin * K_PART, K_PART), :]
            moves.append(remote(part, part, sent_sem.at[1], y_recv.at[1], y_ways[i]))
        return moves

    def start(moves):
        for copy in moves:
            copy.start()

    start(hop_z(1))
    for copy in weights:
        copy.start()

    lane = lax.broadcasted_iota(jnp.int32, (Q_PART, LANES), 1)
    row = lax.broadcasted_iota(jnp.int32, (Q_PART, LANES), 0)
    lane_k = lax.broadcasted_iota(jnp.int32, (K_PART, LANES), 1)

    def prepare_q(place):
        part = z_at(place)
        at_rows = rows(part * Q_PART, Q_PART)
        queries = q[at_rows, :].astype(F32) * 0.125
        turned = pltpu.roll(queries, LANES // 2, 1)
        grads = g[at_rows, :].astype(F32)
        extra = aux[part].astype(F32)
        for h in range(2):
            head = lane // 64 == h
            columns = jnp.concatenate([extra if h else pltpu.roll(extra, 64, 1)] * PAIRS, axis=0)
            source = (lane % 64) // 4 == row // Q_OWN
            less_norm = jnp.where(jnp.logical_and(source, lane % 4 == h), columns, 0.0)
            less_delta = jnp.where(jnp.logical_and(source, lane % 4 == 2 + h), columns, 0.0)
            qa[h, at_rows, :] = jnp.where(head, queries, less_norm).astype(BF)
            ga[h, at_rows, :] = jnp.where(head, grads, less_delta).astype(BF)
            gm[h, at_rows, :] = jnp.where(head, grads, 0.0).astype(BF)
            qr[h, at_rows, :] = jnp.where(head, 0.0, turned).astype(BF)

    def prepare_k(place):
        at_rows = rows(y_at(place) * K_PART, K_PART)
        keys = k[at_rows, :].astype(F32)
        values = v[at_rows, :].astype(F32)
        kt[:, at_rows] = (keys * 0.125).T.astype(BF)
        for h in range(2):
            ks[h, at_rows, :] = jnp.where(lane_k // 64 == h, keys, 1.0).astype(BF)
            vs[h, at_rows, :] = jnp.where(lane_k // 64 == h, values, 1.0).astype(BF)

    def attend(items):
        made = []
        for h, qp, kp in items:
            at_q, at_k = rows(z_at(qp) * Q_PART, Q_PART), rows(y_at(kp) * K_PART, K_PART)
            scores = dot(ks[h, at_k, :], qa[h, at_q, :], NT)
            grads = dot(vs[h, at_k, :], ga[h, at_q, :], NT)
            probs = jnp.exp(scores)
            made.append((h, qp, kp, at_q, at_k, probs.astype(BF), (probs * grads).astype(BF)))
        by_keys, by_queries = {}, {}
        for item in made:
            by_keys.setdefault((item[0], str(item[2])), []).append(item)
            by_queries.setdefault((item[0], str(item[1])), []).append(item)
        for group in by_keys.values():
            h, at_k = group[0][0], group[0][4]
            left = jnp.concatenate([part for item in group for part in item[5:7]], axis=1)
            right = jnp.concatenate(
                [part for item in group for part in (gm[h, item[3], :], qr[h, item[3], :])], axis=0
            )
            acc[h, at_k, :] += dot(left, right, NN)
        for group in by_queries.values():
            h, at_q = group[0][0], group[0][3]
            head = pl.ds(h * 64, 64)
            left = jnp.concatenate([kt[head, item[4]] for item in group], axis=1)
            right = jnp.concatenate([item[6] for item in group], axis=0)
            dqt[head, at_q] += dot(left, right, NN)

    def loop(count, body):
        def step(i, _):
            body(i)
            return 0

        lax.fori_loop(0, count, step, 0)

    def both(qp, kp):
        attend([(0, qp, kp), (1, qp, kp)])

    def give_q(h, place):
        at_rows = rows(z_at(place) * Q_PART, Q_PART)
        return remote(
            send_q.at[h, :, at_rows], got_q.at[h, place - 1],
            sent_sem.at[2], rq_recv.at[h], to_z(z_at(place)),
        )

    def give_k(h, place):
        at_rows = rows(y_at(place) * K_PART, K_PART)
        return remote(
            send_kv.at[h, at_rows, :], got_kv.at[h, place - 1],
            sent_sem.at[2], rkv_recv.at[h], to_y(y_at(place)),
        )

    def finish_q(h, place):
        at_rows = rows(z_at(place) * Q_PART, Q_PART)
        send_q[h, :, at_rows] = dqt[pl.ds(h * 64, 64), at_rows].astype(BF)
        give_q(h, place).start()

    def finish_k(h, place):
        at_rows = rows(y_at(place) * K_PART, K_PART)
        send_kv[h, at_rows, :] = acc[h, at_rows, :].astype(BF)
        give_k(h, place).start()

    hop_rows = 2 * (2 * Q_PART + Q_OWN)
    prepare_q(0)
    prepare_k(0)
    both(0, 0)
    landed(z_recv.at[0], hop_rows)
    start(hop_z(2))
    loop(2, lambda i: prepare_q(i + 1))
    loop(2, lambda i: both(i + 1, 0))
    landed(y_recv.at[0], 4 * K_PART)
    start(hop_y())
    loop(2, lambda i: prepare_k(i + 1))
    loop(3, lambda i: both(i, 1))
    landed(z_recv.at[1], hop_rows)
    start(hop_z(3))
    loop(3, lambda i: both(i, 2))
    loop(2, lambda i: prepare_q(i + 3))
    loop(3, lambda i: attend([(0, 3, i), (0, 4, i)]))
    landed(y_recv.at[1], 2 * K_PART)
    prepare_k(3)
    loop(3, lambda i: both(i, 3))
    landed(z_recv.at[2], hop_rows)
    start(hop_z(4))
    loop(2, lambda i: both(i + 3, 3))
    loop(2, lambda i: prepare_q(i + 5))
    landed(z_recv.at[3], 2 * Q_PART + Q_OWN)
    prepare_q(7)

    def last_of_0(i):
        place = 3 - i
        attend([(0, 5, place), (0, 6, place), (0, 7, place)])

        @pl.when(place > 0)
        def _():
            finish_k(0, place)

    loop(4, last_of_0)
    loop(7, lambda i: finish_q(0, 7 - i))
    attend([(1, 5, 3), (1, 6, 3), (1, 7, 3)])
    finish_k(1, 3)
    loop(2, lambda i: finish_q(1, 2 - i))
    attend([(1, i, 1) for i in range(3, 8)])
    finish_k(1, 1)

    def last_of_1(i):
        place = 7 - i
        attend([(1, place, 2), (1, place, 0)])
        finish_q(1, place)

    loop(3, last_of_1)
    attend([(1, 4, 2), (1, 3, 2)])
    finish_k(1, 2)

    def give_back(i, src, dst):
        for dx, dc in OTHERS:
            to = (x + dx) % NX * NC + (c + dc) % NC
            remote(src(to), dst.at[:, mine], sent_sem.at[3], b_recv.at[i], side(dx, dc)).start()
        copy = pltpu.make_async_copy(src(me), dst.at[:, mine], own_sem.at[i])
        copy.start()
        return copy

    own_q, own_k = rows(z * Q_PART, Q_PART), rows(y * K_PART, K_PART)

    def total_q(h):
        landed(rq_recv.at[h], (NZ - 1) * Q_PART // 2)
        total = dqt[pl.ds(h * 64, 64), own_q]
        for i in range(NZ - 1):
            total += got_q[h, i].astype(F32)
        return total

    def back_k(h):
        landed(rkv_recv.at[h], (NY - 1) * K_PART)
        total = acc[h, own_k, :]
        for i in range(NY - 1):
            total += got_kv[h, i].astype(F32)
        sum_kv[h] = total.astype(BF)
        return give_back(1 + h, lambda to: sum_kv.at[h, rows(to * K_OWN, K_OWN), :], full_kv.at[h])

    back_0 = back_k(0)
    dqt[pl.ds(0, 64), own_q] = total_q(0)
    attend([(1, 4, 0), (1, 3, 0)])
    finish_q(1, 4)
    finish_q(1, 3)
    sum_q[...] = jnp.concatenate([dqt[pl.ds(0, 64), own_q], total_q(1)], axis=0).T.astype(BF)
    back_q = give_back(0, lambda to: sum_q.at[rows(to * Q_OWN, Q_OWN), :], full_q)
    back_1 = back_k(1)

    z_rows = 2 * (NZ - 1) * Q_PART + (NZ - 1) * Q_OWN
    landed(sent_sem.at[0], (PAIRS - 1) * per_peer + z_rows)
    landed(sent_sem.at[1], 2 * (NY - 1) * K_PART)
    landed(sent_sem.at[2], (NZ - 1) * Q_PART + 2 * (NY - 1) * K_PART)
    landed(sent_sem.at[3], (PAIRS - 1) * (Q_OWN + 2 * K_OWN))
    for copy in weights:
        copy.wait()
    back_q.wait()
    landed(b_recv.at[0], (PAIRS - 1) * Q_OWN)
    out_q[...] = dot(full_q[...], wq[...], NT).astype(BF)
    for h, copy in enumerate([back_0, back_1]):
        copy.wait()
        landed(b_recv.at[1 + h], (PAIRS - 1) * K_OWN)
    low = lax.broadcasted_iota(jnp.int32, full_kv.shape[1:], 1) % LANES < 64
    first, second = full_kv[0].astype(F32), full_kv[1].astype(F32)
    width = first.shape[1]
    grad_k = jnp.where(low, pltpu.roll(first, width - 64, 1), pltpu.roll(second, 64, 1)).astype(BF)
    grad_v = jnp.where(low, first, second).astype(BF)
    out_kv[...] = (dot(grad_k, wk[...], NT) + dot(grad_v, wv[...], NT)).astype(BF)


def local(query_saved, key_saved, value_saved, out_grad, log_norm, row_delta, wq, wk, wv):
    width = query_saved.shape[1]
    hbm, vmem = pl.BlockSpec(memory_space=pl.ANY), pl.BlockSpec(memory_space=pltpu.VMEM)
    dma = pltpu.SemaphoreType.DMA
    return pl.pallas_call(
        kernel,
        out_shape=(
            jax.ShapeDtypeStruct((Q_OWN, width), BF),
            jax.ShapeDtypeStruct((K_OWN, width), BF),
        ),
        in_specs=[hbm] * 9,
        out_specs=(vmem, vmem),
        scratch_shapes=[
            pltpu.VMEM((Q_ALL, LANES), BF), pltpu.VMEM((Q_ALL, LANES), BF),
            pltpu.VMEM((K_ALL, LANES), BF), pltpu.VMEM((K_ALL, LANES), BF),
            pltpu.VMEM(log_norm.shape, BF), pltpu.VMEM(row_delta.shape, BF),
            pltpu.VMEM((Q_OWN, width), BF), pltpu.VMEM((PAIRS, Q_OWN, LANES), BF),
            pltpu.VMEM((NZ, Q_OWN, LANES), BF),
            *[pltpu.VMEM((2, Q_ALL, LANES), BF)] * 4, *[pltpu.VMEM((2, K_ALL, LANES), BF)] * 2,
            pltpu.VMEM((LANES, K_ALL), BF), pltpu.VMEM((LANES, Q_ALL), F32),
            pltpu.VMEM((2, K_ALL, LANES), F32),
            pltpu.VMEM((2, 64, Q_ALL), BF), pltpu.VMEM((2, K_ALL, LANES), BF),
            pltpu.VMEM((2, NZ - 1, 64, Q_PART), BF), pltpu.VMEM((2, NY - 1, K_PART, LANES), BF),
            pltpu.VMEM((Q_PART, LANES), BF), pltpu.VMEM((2, K_PART, LANES), BF),
            pltpu.VMEM((Q_OWN, width), BF), pltpu.VMEM((2, K_OWN, width), BF),
            *[pltpu.VMEM((width, width), BF)] * 3,
            pltpu.VMEM((8192, LANES), BF),
            dma((6,)), dma((3,)), dma((4,)), dma((NX,)), dma((NZ // 2,)), dma((2,)),
            dma((2,)), dma((2,)), dma((3,)),
        ],
        compiler_params=pltpu.CompilerParams(
            collective_id=0, has_side_effects=True, vmem_limit_bytes=60 * 2**20
        ),
        name="attention_backward",
    )(query_saved, key_saved, value_saved, out_grad, log_norm, row_delta, wq, wk, wv)


def solution(mesh):
    in_specs = (
        P(("pb", "ka"), None),
        P(("ka", "pb"), None),
        P(("ka", "pb"), None),
        P(("pb", "ka"), None),
        P(None, ("pb", "ka")),
        P(None, ("pb", "ka")),
        P(),
        P(),
        P(),
    )
    out_specs = (P(("pb", "ka"), None), P(("ka", "pb"), None))
    return jax.shard_map(local, mesh=mesh, in_specs=in_specs, out_specs=out_specs, check_vma=False)
```

time: 68.7 us -> 65.2 us (0.949)
  Pallas kernels: 64.9 us -> 61.3 us
    pallas_call x1, Pallas kernels: 64.9 us -> 61.3 us  [local(): pl.pallas_call(kernel, out_shape=(jax.ShapeDtypeStruct((Q_OWN, width), BF...]
where the time goes in v3:
time: 65.2 us; the launch traced here: 65 us
  Pallas kernels  61.3 us (94%)
  local copies, waits for them, and re-layouts  3.04 us (5%)
    pallas_call x1, Pallas kernels, local(): pl.pallas_call(kernel, out_shape=(jax.ShapeDtypeStruct((Q_OWN, width), BF...  61.3 us
    unnamed x2, local copies, waits for them, and re-layouts  3.04 us

profile of v3, /device:TPU:1, one launch (start us, length us, event | category | flops | bytes accessed | tf_op | source)
XLA Modules:
  0.0 65.0 jit_solution(12845514105218389960)
XLA Ops:
  0.6 61.3 %attention_backward.1 = (bf16[32,1024]{1,0:T(8,128)(2,1)}, bf16[64,1024]{1,0:T(8,128)(2,1)}) custom-call(bf16[32,1024]{1,0:T(8,128)(2,1)} %q_hbm.1, bf16[64,1024]{1,0:T(8,128)(2,1)} %k_hbm.1, bf16[64,1024]{1,0:T(8,128)(2,1)} %v_hbm.1, bf16[32,1024]{1,0:T(8,128)(2,1)} %g_hbm.1, bf16[16,32]{1,0:T(8,128)(2,1)} %norm_hbm.1, bf16[16,32]{1,0:T(8,128)(2,1)} %delta_hbm.1, ...), custom_call_target="tpu_custom_call" | custom-call | tf_op jit(solution)/shard_map/attention_backward/pallas_call | solution.py:375
  62.0 1.5 %copy.13 = bf16[32,1024]{1,0:T(8,128)(2,1)} copy(bf16[32,1024]{1,0:T(8,128)(2,1)} %get-tuple-element.4) | data formatting | bytes 131072
  63.4 1.6 %copy.14 = bf16[64,1024]{1,0:T(8,128)(2,1)} copy(bf16[64,1024]{1,0:T(8,128)(2,1)} %get-tuple-element.5) | data formatting | bytes 262144

commit v4 on v3

--- a/solution.py
+++ b/solution.py
@@ -28,13 +28,12 @@
 
 
 def kernel(
-    q_hbm, k_hbm, v_hbm, g_hbm, norm_hbm, delta_hbm, wq_hbm, wk_hbm, wv_hbm,
-    out_q, out_kv,
+    q_hbm, k_hbm, v_hbm, g_hbm, norm_hbm, delta_hbm,
+    full_q, full_kv,
     q, g, k, v, norm, delta, aux_out, aux_in, aux,
     qa, qr, ga, gm, ks, vs, kt, dqt, acc,
-    send_q, send_kv, got_q, got_kv, sum_q, sum_kv, full_q, full_kv,
-    wq, wk, wv, tally,
-    own_sem, w_sem, sent_sem, a_recv, z_recv, y_recv, rq_recv, rkv_recv, b_recv,
+    send_q, send_kv, got_q, got_kv, sum_q, sum_kv, tally,
+    own_sem, sent_sem, a_recv, z_recv, y_recv, rq_recv, rkv_recv, b_recv,
 ):
     pb, ka = lax.axis_index("pb"), lax.axis_index("ka")
     z, y, c = pb % NZ, (ka // NC) % NY, ka % NC
@@ -115,10 +114,6 @@
                 remote(src.at[:, cols], dst.at[at_rows, :], sent_sem.at[0], a_recv.at[dx], side(dx, dc)).start()
             remote(aux_out.at[:, cols], aux_in.at[j], sent_sem.at[0], a_recv.at[dx], side(dx, dc)).start()
     per_peer = 3 * Q_OWN + 2 * K_OWN
-    weights = [
-        pltpu.make_async_copy(src, dst, w_sem.at[i])
-        for i, (src, dst) in enumerate([(wq_hbm, wq), (wk_hbm, wk), (wv_hbm, wv)])
-    ]
 
     z_ways = [to_z(z_at(1)), to_z(z_at(2))]
     y_ways = [to_y(y_at(1)), to_y(y_at(2))]
@@ -167,8 +162,6 @@
             copy.start()
 
     start(hop_z(1))
-    for copy in weights:
-        copy.start()
 
     lane = lax.broadcasted_iota(jnp.int32, (Q_PART, LANES), 1)
     row = lax.broadcasted_iota(jnp.int32, (Q_PART, LANES), 0)
@@ -234,8 +227,8 @@
 
         lax.fori_loop(0, count, step, 0)
 
-    def both(qp, kp):
-        attend([(0, qp, kp), (1, qp, kp)])
+    def both(qps, kp):
+        attend([(h, qp, kp) for h in range(2) for qp in qps])
 
     def give_q(h, place):
         at_rows = rows(z_at(place) * Q_PART, Q_PART)
@@ -264,27 +257,31 @@
     hop_rows = 2 * (2 * Q_PART + Q_OWN)
     prepare_q(0)
     prepare_k(0)
-    both(0, 0)
+    both([0], 0)
     landed(z_recv.at[0], hop_rows)
     start(hop_z(2))
-    loop(2, lambda i: prepare_q(i + 1))
-    loop(2, lambda i: both(i + 1, 0))
+    prepare_q(1)
+    prepare_q(2)
+    both([1, 2], 0)
     landed(y_recv.at[0], 4 * K_PART)
     start(hop_y())
-    loop(2, lambda i: prepare_k(i + 1))
-    loop(3, lambda i: both(i, 1))
+    prepare_k(1)
+    both([0, 1, 2], 1)
+    prepare_k(2)
     landed(z_recv.at[1], hop_rows)
     start(hop_z(3))
-    loop(3, lambda i: both(i, 2))
-    loop(2, lambda i: prepare_q(i + 3))
-    loop(3, lambda i: attend([(0, 3, i), (0, 4, i)]))
+    both([0, 1, 2], 2)
+    prepare_q(3)
+    prepare_q(4)
+    attend([(0, qp, kp) for kp in range(3) for qp in (3, 4)])
     landed(y_recv.at[1], 2 * K_PART)
     prepare_k(3)
-    loop(3, lambda i: both(i, 3))
+    both([0, 1, 2], 3)
     landed(z_recv.at[2], hop_rows)
     start(hop_z(4))
-    loop(2, lambda i: both(i + 3, 3))
-    loop(2, lambda i: prepare_q(i + 5))
+    both([3, 4], 3)
+    prepare_q(5)
+    prepare_q(6)
     landed(z_recv.at[3], 2 * Q_PART + Q_OWN)
     prepare_q(7)
 
@@ -352,14 +349,15 @@
     landed(sent_sem.at[1], 2 * (NY - 1) * K_PART)
     landed(sent_sem.at[2], (NZ - 1) * Q_PART + 2 * (NY - 1) * K_PART)
     landed(sent_sem.at[3], (PAIRS - 1) * (Q_OWN + 2 * K_OWN))
-    for copy in weights:
-        copy.wait()
     back_q.wait()
     landed(b_recv.at[0], (PAIRS - 1) * Q_OWN)
-    out_q[...] = dot(full_q[...], wq[...], NT).astype(BF)
     for h, copy in enumerate([back_0, back_1]):
         copy.wait()
         landed(b_recv.at[1 + h], (PAIRS - 1) * K_OWN)
+
+
+def project(full_q, full_kv, wq, wk, wv, out_q, out_kv):
+    out_q[...] = dot(full_q[...], wq[...], NT).astype(BF)
     low = lax.broadcasted_iota(jnp.int32, full_kv.shape[1:], 1) % LANES < 64
     first, second = full_kv[0].astype(F32), full_kv[1].astype(F32)
     width = first.shape[1]
@@ -370,15 +368,15 @@
 
 def local(query_saved, key_saved, value_saved, out_grad, log_norm, row_delta, wq, wk, wv):
     width = query_saved.shape[1]
-    hbm, vmem = pl.BlockSpec(memory_space=pl.ANY), pl.BlockSpec(memory_space=pltpu.VMEM)
+    hbm, vmem = pl.BlockSpec(memory_space=pltpu.HBM), pl.BlockSpec(memory_space=pltpu.VMEM)
     dma = pltpu.SemaphoreType.DMA
-    return pl.pallas_call(
+    full_q, full_kv = pl.pallas_call(
         kernel,
         out_shape=(
             jax.ShapeDtypeStruct((Q_OWN, width), BF),
-            jax.ShapeDtypeStruct((K_OWN, width), BF),
+            jax.ShapeDtypeStruct((2, K_OWN, width), BF),
         ),
-        in_specs=[hbm] * 9,
+        in_specs=[hbm] * 6,
         out_specs=(vmem, vmem),
         scratch_shapes=[
             pltpu.VMEM((Q_ALL, LANES), BF), pltpu.VMEM((Q_ALL, LANES), BF),
@@ -392,17 +390,29 @@
             pltpu.VMEM((2, 64, Q_ALL), BF), pltpu.VMEM((2, K_ALL, LANES), BF),
             pltpu.VMEM((2, NZ - 1, 64, Q_PART), BF), pltpu.VMEM((2, NY - 1, K_PART, LANES), BF),
             pltpu.VMEM((Q_PART, LANES), BF), pltpu.VMEM((2, K_PART, LANES), BF),
-            pltpu.VMEM((Q_OWN, width), BF), pltpu.VMEM((2, K_OWN, width), BF),
-            *[pltpu.VMEM((width, width), BF)] * 3,
             pltpu.VMEM((8192, LANES), BF),
-            dma((6,)), dma((3,)), dma((4,)), dma((NX,)), dma((NZ // 2,)), dma((2,)),
+            dma((6,)), dma((4,)), dma((NX,)), dma((NZ // 2,)), dma((2,)),
             dma((2,)), dma((2,)), dma((3,)),
         ],
         compiler_params=pltpu.CompilerParams(
-            collective_id=0, has_side_effects=True, vmem_limit_bytes=60 * 2**20
+            collective_id=0, has_side_effects=True, vmem_limit_bytes=40 * 2**20
+        ),
+        cost_estimate=pl.CostEstimate(
+            flops=20 * Q_ALL * K_ALL * 64, bytes_accessed=2**20, transcendentals=2 * Q_ALL * K_ALL
         ),
         name="attention_backward",
-    )(query_saved, key_saved, value_saved, out_grad, log_norm, row_delta, wq, wk, wv)
+    )(*[pltpu.with_memory_space_constraint(a, pltpu.HBM) for a in (query_saved, key_saved, value_saved, out_grad, log_norm, row_delta)])
+    return pl.pallas_call(
+        project,
+        out_shape=(
+            jax.ShapeDtypeStruct((Q_OWN, width), BF),
+            jax.ShapeDtypeStruct((K_OWN, width), BF),
+        ),
+        in_specs=[vmem] * 5,
+        out_specs=(vmem, vmem),
+        compiler_params=pltpu.CompilerParams(vmem_limit_bytes=16 * 2**20),
+        name="projections",
+    )(full_q, full_kv, wq, wk, wv)
 
 
 def solution(mesh):

time: 65.2 us -> 61.4 us (0.942)
  local copies, waits for them, and re-layouts: 3.04 us -> 0.01 us
  Pallas kernels: 61.3 us -> 60.6 us
    pallas_call x1, Pallas kernels: 61.3 us -> 57.9 us  [local(): pl.pallas_call(kernel, out_shape=(jax.ShapeDtypeStruct((Q_OWN, width), BF...]
    unnamed x2 -> x6, local copies, waits for them, and re-layouts: 3.04 us -> 0.01 us
    pallas_call x0 -> x1, Pallas kernels: none -> 2.66 us  [local(): pl.pallas_call(project, out_shape=(jax.ShapeDtypeStruct((Q_OWN, width), B...]
where the time goes in v4:
time: 61.4 us; the launch traced here: 61.3 us
  Pallas kernels  60.6 us (99%)
  between operations  0.69 us (1%)
    pallas_call x1, Pallas kernels, local(): pl.pallas_call(kernel, out_shape=(jax.ShapeDtypeStruct((Q_OWN, width), BF...  57.9 us
    pallas_call x1, Pallas kernels, local(): pl.pallas_call(project, out_shape=(jax.ShapeDtypeStruct((Q_OWN, width), B...  2.66 us

profile of v4, /device:TPU:1, one launch (start us, length us, event | category | flops | bytes accessed | tf_op | source)
XLA Modules:
  0.0 61.3 jit_solution(13097038074917956657)
XLA Ops:
  0.6 0.0 copy-start.2
  0.6 0.0 copy-start.1
  0.7 0.0 copy-start
  0.7 57.9 %attention_backward.1 = (bf16[32,1024]{1,0:T(8,128)(2,1)S(1)}, bf16[2,64,1024]{2,1,0:T(8,128)(2,1)S(1)}) custom-call(bf16[32,1024]{1,0:T(8,128)(2,1)} %q_hbm.1, bf16[64,1024]{1,0:T(8,128)(2,1)} %k_hbm.1, bf16[64,1024]{1,0:T(8,128)(2,1)} %v_hbm.1, bf16[32,1024]{1,0:T(8,128)(2,1)} %g_hbm.1, bf16[16,32]{1,0:T(8,128)(2,1)} %norm_hbm.1, bf16[16,32]{1,0:T(8,128)(2,1)} %delta_hbm.1), custom_call_target="tpu_custom_call" | custom-call | flops 5368709120 | bytes 1048576 | tf_op jit(solution)/shard_map/attention_backward/pallas_call | solution.py:373
  58.6 0.0 copy-done.2
  58.6 0.0 copy-done.1
  58.6 0.0 copy-done
  58.6 2.7 %projections.1 = (bf16[32,1024]{1,0:T(8,128)(2,1)}, bf16[64,1024]{1,0:T(8,128)(2,1)}) custom-call(bf16[32,1024]{1,0:T(8,128)(2,1)S(1)} %get-tuple-element.4.full_q, bf16[2,64,1024]{2,1,0:T(8,128)(2,1)S(1)} %get-tuple-element.5.full_kv, bf16[1024,1024]{1,0:T(8,128)(2,1)S(1)} %copy-done, bf16[1024,1024]{1,0:T(8,128)(2,1)S(1)} %copy-done.1, ...), custom_call_target="tpu_custom_call" | custom-call | tf_op jit(solution)/shard_map/projections/pallas_call | solution.py:405
Async XLA Ops:
  0.6 58.0 %copy-start.2 = (bf16[1024,1024]{1,0:T(8,128)(2,1)S(1)}, bf16[1024,1024]{1,0:T(8,128)(2,1)}, u32[]{:S(2)}) copy-start(bf16[1024,1024]{1,0:T(8,128)(2,1)} %wv.1) | copy-start | bytes 6291460
  0.6 58.0 %copy-start.1 = (bf16[1024,1024]{1,0:T(8,128)(2,1)S(1)}, bf16[1024,1024]{1,0:T(8,128)(2,1)}, u32[]{:S(2)}) copy-start(bf16[1024,1024]{1,0:T(8,128)(2,1)} %wk.1) | copy-start | bytes 6291460
  0.7 58.0 %copy-start = (bf16[1024,1024]{1,0:T(8,128)(2,1)S(1)}, bf16[1024,1024]{1,0:T(8,128)(2,1)}, u32[]{:S(2)}) copy-start(bf16[1024,1024]{1,0:T(8,128)(2,1)} %wq.1) | copy-start | bytes 6291460

commit v5 on v4

--- a/solution.py
+++ b/solution.py
@@ -33,7 +33,7 @@
     q, g, k, v, norm, delta, aux_out, aux_in, aux,
     qa, qr, ga, gm, ks, vs, kt, dqt, acc,
     send_q, send_kv, got_q, got_kv, sum_q, sum_kv, tally,
-    own_sem, sent_sem, a_recv, z_recv, y_recv, rq_recv, rkv_recv, b_recv,
+    own_sem, sent_sem, a_recv, ak_recv, z_recv, y_recv, rq_recv, rkv_recv, b_recv,
 ):
     pb, ka = lax.axis_index("pb"), lax.axis_index("ka")
     z, y, c = pb % NZ, (ka // NC) % NY, ka % NC
@@ -104,32 +104,42 @@
     dqt[...] = jnp.zeros_like(dqt)
     pl.semaphore_wait(barrier, len(peers))
 
-    for dx in (0, 1, 3, 2):
-        for dc in range(NC):
-            if not (dx or dc):
-                continue
-            j = dx * NC + dc
-            cols = rows(((x + dx) % NX * NC + (c + dc) % NC) * LANES, LANES)
-            for src, dst, at_rows in exchanged:
-                remote(src.at[:, cols], dst.at[at_rows, :], sent_sem.at[0], a_recv.at[dx], side(dx, dc)).start()
-            remote(aux_out.at[:, cols], aux_in.at[j], sent_sem.at[0], a_recv.at[dx], side(dx, dc)).start()
+    def exchange(arrays, arrived):
+        for dx in (0, 1, 3, 2):
+            for dc in range(NC):
+                if not (dx or dc):
+                    continue
+                j = dx * NC + dc
+                cols = rows(((x + dx) % NX * NC + (c + dc) % NC) * LANES, LANES)
+                for src, dst, at_rows in arrays:
+                    to = dst.at[j] if at_rows is None else dst.at[at_rows, :]
+                    remote(src.at[:, cols], to, sent_sem.at[0], arrived.at[dx], side(dx, dc)).start()
+
+    exchange(exchanged[:2] + [(aux_out, aux_in, None)], a_recv)
+    exchange(exchanged[2:], ak_recv)
     per_peer = 3 * Q_OWN + 2 * K_OWN
 
     z_ways = [to_z(z_at(1)), to_z(z_at(2))]
     y_ways = [to_y(y_at(1)), to_y(y_at(2))]
     for dx in (0, 1, 3, 2):
-        landed(a_recv.at[dx], per_peer * (NC if dx else NC - 1))
+        landed(a_recv.at[dx], 3 * Q_OWN * (NC if dx else NC - 1))
         from_x = (x - dx + NX) % NX
         at_q = rows(z * Q_PART + from_x * NC * Q_OWN, NC * Q_OWN)
+        for buf in (q, g):
+            for d in range(2):
+                part = buf.at[at_q, :]
+                remote(part, part, sent_sem.at[0], z_recv.at[0], z_ways[d]).start()
+
+    def first_y(dx):
+        landed(ak_recv.at[dx], 2 * K_OWN * (NC if dx else NC - 1))
+        from_x = (x - dx + NX) % NX
         at_k = rows(y * K_PART + from_x * NC * K_OWN, NC * K_OWN)
         for buf in (k, v):
             for d in range(2):
                 part = buf.at[at_k, :]
                 remote(part, part, sent_sem.at[1], y_recv.at[0], y_ways[d]).start()
-        for buf in (q, g):
-            for d in range(2):
-                part = buf.at[at_q, :]
-                remote(part, part, sent_sem.at[0], z_recv.at[0], z_ways[d]).start()
+
+    first_y(0)
     aux_sum = aux_out[:, mine].astype(F32)
     for dx, dc in OTHERS:
         aux_sum += aux_in[dx * NC + dc].astype(F32)
@@ -162,6 +172,8 @@
             copy.start()
 
     start(hop_z(1))
+    for dx in (1, 3, 2):
+        first_y(dx)
 
     lane = lax.broadcasted_iota(jnp.int32, (Q_PART, LANES), 1)
     row = lax.broadcasted_iota(jnp.int32, (Q_PART, LANES), 0)
@@ -263,22 +275,23 @@
     prepare_q(1)
     prepare_q(2)
     both([1, 2], 0)
+    landed(z_recv.at[1], hop_rows)
+    start(hop_z(3))
+    prepare_q(3)
+    prepare_q(4)
+    both([3, 4], 0)
     landed(y_recv.at[0], 4 * K_PART)
     start(hop_y())
     prepare_k(1)
     both([0, 1, 2], 1)
     prepare_k(2)
-    landed(z_recv.at[1], hop_rows)
-    start(hop_z(3))
     both([0, 1, 2], 2)
-    prepare_q(3)
-    prepare_q(4)
-    attend([(0, qp, kp) for kp in range(3) for qp in (3, 4)])
+    landed(z_recv.at[2], hop_rows)
+    start(hop_z(4))
+    attend([(0, qp, kp) for kp in (1, 2) for qp in (3, 4)])
     landed(y_recv.at[1], 2 * K_PART)
     prepare_k(3)
     both([0, 1, 2], 3)
-    landed(z_recv.at[2], hop_rows)
-    start(hop_z(4))
     both([3, 4], 3)
     prepare_q(5)
     prepare_q(6)
@@ -301,14 +314,13 @@
     attend([(1, i, 1) for i in range(3, 8)])
     finish_k(1, 1)
 
-    def last_of_1(i):
-        place = 7 - i
-        attend([(1, place, 2), (1, place, 0)])
-        finish_q(1, place)
-
-    loop(3, last_of_1)
-    attend([(1, 4, 2), (1, 3, 2)])
+    attend([(1, qp, kp) for qp in (7, 6) for kp in (2, 0)])
+    finish_q(1, 7)
+    finish_q(1, 6)
+    attend([(1, 5, 2), (1, 4, 2), (1, 3, 2)])
     finish_k(1, 2)
+    finish_q(1, 4)
+    finish_q(1, 3)
 
     def give_back(i, src, dst):
         for dx, dc in OTHERS:
@@ -335,11 +347,10 @@
         sum_kv[h] = total.astype(BF)
         return give_back(1 + h, lambda to: sum_kv.at[h, rows(to * K_OWN, K_OWN), :], full_kv.at[h])
 
+    attend([(1, 5, 0)])
+    finish_q(1, 5)
     back_0 = back_k(0)
     dqt[pl.ds(0, 64), own_q] = total_q(0)
-    attend([(1, 4, 0), (1, 3, 0)])
-    finish_q(1, 4)
-    finish_q(1, 3)
     sum_q[...] = jnp.concatenate([dqt[pl.ds(0, 64), own_q], total_q(1)], axis=0).T.astype(BF)
     back_q = give_back(0, lambda to: sum_q.at[rows(to * Q_OWN, Q_OWN), :], full_q)
     back_1 = back_k(1)
@@ -391,7 +402,7 @@
             pltpu.VMEM((2, NZ - 1, 64, Q_PART), BF), pltpu.VMEM((2, NY - 1, K_PART, LANES), BF),
             pltpu.VMEM((Q_PART, LANES), BF), pltpu.VMEM((2, K_PART, LANES), BF),
             pltpu.VMEM((8192, LANES), BF),
-            dma((6,)), dma((4,)), dma((NX,)), dma((NZ // 2,)), dma((2,)),
+            dma((6,)), dma((4,)), dma((NX,)), dma((NX,)), dma((NZ // 2,)), dma((2,)),
             dma((2,)), dma((2,)), dma((3,)),
         ],
         compiler_params=pltpu.CompilerParams(

time: 61.4 us -> 59.7 us (0.972)
  Pallas kernels: 60.6 us -> 58.9 us
    pallas_call x1, Pallas kernels: 57.9 us -> 56.3 us  [local(): pl.pallas_call(kernel, out_shape=(jax.ShapeDtypeStruct((Q_OWN, width), BF...]
where the time goes in v5:
time: 59.7 us; the launch traced here: 59.6 us
  Pallas kernels  58.9 us (99%)
  between operations  0.69 us (1%)
    pallas_call x1, Pallas kernels, local(): pl.pallas_call(kernel, out_shape=(jax.ShapeDtypeStruct((Q_OWN, width), BF...  56.3 us
    pallas_call x1, Pallas kernels, local(): pl.pallas_call(project, out_shape=(jax.ShapeDtypeStruct((Q_OWN, width), B...  2.66 us

profile of v5, /device:TPU:1, one launch (start us, length us, event | category | flops | bytes accessed | tf_op | source)
XLA Modules:
  0.0 59.6 jit_solution(8593624106794302840)
XLA Ops:
  0.6 0.0 copy-start.2
  0.6 0.0 copy-start.1
  0.7 0.0 copy-start
  0.7 56.3 %attention_backward.1 = (bf16[32,1024]{1,0:T(8,128)(2,1)S(1)}, bf16[2,64,1024]{2,1,0:T(8,128)(2,1)S(1)}) custom-call(bf16[32,1024]{1,0:T(8,128)(2,1)} %q_hbm.1, bf16[64,1024]{1,0:T(8,128)(2,1)} %k_hbm.1, bf16[64,1024]{1,0:T(8,128)(2,1)} %v_hbm.1, bf16[32,1024]{1,0:T(8,128)(2,1)} %g_hbm.1, bf16[16,32]{1,0:T(8,128)(2,1)} %norm_hbm.1, bf16[16,32]{1,0:T(8,128)(2,1)} %delta_hbm.1), custom_call_target="tpu_custom_call" | custom-call | flops 5368709120 | bytes 1048576 | tf_op jit(solution)/shard_map/attention_backward/pallas_call | solution.py:384
  56.9 0.0 copy-done.2
  56.9 0.0 copy-done.1
  57.0 0.0 copy-done
  57.0 2.7 %projections.1 = (bf16[32,1024]{1,0:T(8,128)(2,1)}, bf16[64,1024]{1,0:T(8,128)(2,1)}) custom-call(bf16[32,1024]{1,0:T(8,128)(2,1)S(1)} %get-tuple-element.4.full_q, bf16[2,64,1024]{2,1,0:T(8,128)(2,1)S(1)} %get-tuple-element.5.full_kv, bf16[1024,1024]{1,0:T(8,128)(2,1)S(1)} %copy-done, bf16[1024,1024]{1,0:T(8,128)(2,1)S(1)} %copy-done.1, ...), custom_call_target="tpu_custom_call" | custom-call | tf_op jit(solution)/shard_map/projections/pallas_call | solution.py:416
Async XLA Ops:
  0.6 56.3 %copy-start.2 = (bf16[1024,1024]{1,0:T(8,128)(2,1)S(1)}, bf16[1024,1024]{1,0:T(8,128)(2,1)}, u32[]{:S(2)}) copy-start(bf16[1024,1024]{1,0:T(8,128)(2,1)} %wv.1) | copy-start | bytes 6291460
  0.6 56.3 %copy-start.1 = (bf16[1024,1024]{1,0:T(8,128)(2,1)S(1)}, bf16[1024,1024]{1,0:T(8,128)(2,1)}, u32[]{:S(2)}) copy-start(bf16[1024,1024]{1,0:T(8,128)(2,1)} %wk.1) | copy-start | bytes 6291460
  0.7 56.3 %copy-start = (bf16[1024,1024]{1,0:T(8,128)(2,1)S(1)}, bf16[1024,1024]{1,0:T(8,128)(2,1)}, u32[]{:S(2)}) copy-start(bf16[1024,1024]{1,0:T(8,128)(2,1)} %wq.1) | copy-start | bytes 6291460
